TPU v7x, 256 devices: a whole 4x4x8 slice. The times are simulated.
256 devices in a mesh: tensor: 4 (over z_lo, core), request: 64 (over x, y, z_hi).
Axes of the slice: x: 4, y: 4, z: 8 (z_hi: 4, z_lo: 2; z = z_hi * 2 + z_lo), core: 2. Of those that a mesh axis runs over, the one named last changes fastest.
Arguments:
- hidden_in: bfloat16 [16384, 2048], P('request'), may hold values from -6 to 6
- span_q: bfloat16 [16384, 2048], P('request', 'tensor'), may hold values from -170 to 170
- span_k: bfloat16 [16384, 2048], P('request', 'tensor'), may hold values from -7 to 7
- span_v: bfloat16 [16384, 2048], P('request', 'tensor'), may hold values from -6 to 6
- cache_k: bfloat16 [64, 768, 2048], P('request', None, 'tensor'), may hold values from -6 to 6
- cache_v: bfloat16 [64, 768, 2048], P('request', None, 'tensor'), may hold values from -6 to 6
- cached_len: int32 [64], P('request'), may hold values from 0 to 768
- out_proj: bfloat16 [2048, 2048], P('tensor'), may hold values from -0.125 to 0.125
- norm_gain: float32 [2048], replicated, may hold values from 0.1 to 1.9
- routes: int32 [16384, 4], P('request'), may hold values from 0 to 63, all different within a row; in each aligned block of 256 rows (0 to 255, 256 to 511, ...) at most 32 rows name the same one
- route_weight: float32 [16384, 4], P('request'), may hold values from 0.1 to 1
- w_gate: bfloat16 [64, 2048, 1408], P('request', None, 'tensor'), may hold values from -0.125 to 0.125
- w_up: bfloat16 [64, 2048, 1408], P('request', None, 'tensor'), may hold values from -0.125 to 0.125
- w_down: bfloat16 [64, 1408, 2048], P('request', 'tensor'), may hold values from -0.15625 to 0.15625
Outputs:
- layer_out: bfloat16 [16384, 2048], P('request', 'tensor')
- decode_kv: bfloat16 [64, 2, 1024, 2048], P('request', None, 'tensor')
Inputs may be any that keep to these rules, and one draw needn't show every extreme that they name: `routes`: among the rows of one request no expert is named more than 32 times.
All inputs are finite; a program needn't handle non-finite values.
Results may differ from a plain program's by a relative error of at most 0.014.
Values may be sent and summed in bfloat16 or wider, within the bound.
No kernel may reach another device: no remote copies, remote signals or barrier semaphores. Data moves between devices by JAX's collectives and lax.ppermute only.
A program may use at most 128 MiB of HBM per device.

v0:
```python
import jax
import jax.numpy as jnp
from jax import lax
from jax.experimental import pallas as pl
from jax.experimental.pallas import tpu as pltpu
from jax.sharding import PartitionSpec as P


HD = 128
TOP = 4
RING = 4


eps = 1e-06
neg_large = -1e30


NT = (((1,), (1,)), ((), ()))
TN = (((0,), (0,)), ((), ()))
VMEM = pl.BlockSpec(memory_space=pltpu.VMEM)
SMEM = pl.BlockSpec(memory_space=pltpu.SMEM)


def lanes(start, size):
    return pl.ds(pl.multiple_of(start, 128), size)


def attend_kernel(
    scalars_ref, q_ref, k_ref, v_ref, ck_ref, cv_ref, w_ref, keep_ref, send_ref, part_ref
):
    head = pl.program_id(0)
    length, core = scalars_ref[0], scalars_ref[1]
    query = q_ref[...]
    scale = HD ** (-0.5)
    old = lax.dot_general(query, ck_ref[...], NT, preferred_element_type=jnp.float32) * scale
    new = lax.dot_general(query, k_ref[...], NT, preferred_element_type=jnp.float32) * scale
    old = jnp.where(lax.broadcasted_iota(jnp.int32, old.shape, 1) < length, old, neg_large)
    rows = lax.broadcasted_iota(jnp.int32, new.shape, 0)
    new = jnp.where(lax.broadcasted_iota(jnp.int32, new.shape, 1) <= rows, new, neg_large)
    top = jnp.maximum(
        jnp.max(old, axis=1, keepdims=True), jnp.max(new, axis=1, keepdims=True)
    )
    old = jnp.exp(old - top)
    new = jnp.exp(new - top)
    inverse = 1.0 / (jnp.sum(old, axis=1, keepdims=True) + jnp.sum(new, axis=1, keepdims=True))
    attended = jnp.dot(
        (old * inverse).astype(jnp.bfloat16), cv_ref[...], preferred_element_type=jnp.float32
    ) + jnp.dot(
        (new * inverse).astype(jnp.bfloat16), v_ref[...], preferred_element_type=jnp.float32
    )
    part = jnp.dot(
        attended.astype(jnp.bfloat16), w_ref[...], preferred_element_type=jnp.float32
    )

    @pl.when(head == 0)
    def _():
        part_ref[...] = part

    @pl.when(head > 0)
    def _():
        part_ref[...] += part

    @pl.when(head == pl.num_programs(0) - 1)
    def _():
        half = keep_ref.shape[1]
        keep_ref[...] = part_ref[:, lanes(core * half, half)]
        send_ref[...] = part_ref[:, lanes((1 - core) * half, half)].astype(jnp.bfloat16)


def attend(scalars, span_q, span_k, span_v, cache_k, cache_v, out_proj):
    span, columns = span_q.shape
    prior = cache_k.shape[0]
    width = out_proj.shape[1]
    heads = columns // HD
    fresh = pl.BlockSpec((span, HD), lambda h, n: (0, h))
    cached = pl.BlockSpec((prior, HD), lambda h, n: (0, h))
    halves = pl.BlockSpec((span, width // 2), lambda h, n: (0, 0))
    return pl.pallas_call(
        attend_kernel,
        grid_spec=pltpu.PrefetchScalarGridSpec(
            num_scalar_prefetch=1,
            grid=(heads,),
            in_specs=[
                fresh,
                fresh,
                fresh,
                cached,
                cached,
                pl.BlockSpec((HD, width), lambda h, n: (h, 0)),
            ],
            out_specs=[halves, halves],
            scratch_shapes=[pltpu.VMEM((span, width), jnp.float32)],
        ),
        out_shape=[
            jax.ShapeDtypeStruct((span, width // 2), jnp.float32),
            jax.ShapeDtypeStruct((span, width // 2), jnp.bfloat16),
        ],
        cost_estimate=pl.CostEstimate(
            flops=heads * span * (4 * (prior + span) * HD + 2 * HD * width),
            transcendentals=heads * span * (prior + span),
            bytes_accessed=9 << 20,
        ),
        name="attend",
    )(scalars, span_q, span_k, span_v, cache_k, cache_v, out_proj)


def norm_kernel(scalars_ref, mine_ref, other_ref, gain_ref, mine_out, other_out, own_out):
    chip, core = scalars_ref[0], scalars_ref[1]
    half = mine_ref.shape[1]
    quarter = half // 2
    mine = mine_ref[...].astype(jnp.float32)
    other = other_ref[...].astype(jnp.float32)
    total = jnp.sum(mine * mine, axis=1, keepdims=True) + jnp.sum(
        other * other, axis=1, keepdims=True
    )
    scale = lax.rsqrt(total / (2 * half) + eps)
    mine_gain = gain_ref[:, lanes(core * half, half)]
    other_gain = gain_ref[:, lanes((1 - core) * half, half)]
    mine_out[...] = (mine * scale * mine_gain).astype(jnp.bfloat16)
    other_out[...] = (other * scale * other_gain).astype(jnp.bfloat16)

    @pl.when(chip == core)
    def _():
        own_out[...] = mine_ref[:, lanes(core * quarter, quarter)]

    @pl.when(chip != core)
    def _():
        own_out[...] = other_ref[:, lanes(core * quarter, quarter)]


def norm(scalars, mine, other, gain):
    span, half = mine.shape
    return pl.pallas_call(
        norm_kernel,
        in_specs=[SMEM, VMEM, VMEM, VMEM],
        out_specs=[VMEM] * 3,
        out_shape=[
            jax.ShapeDtypeStruct((span, half), jnp.bfloat16),
            jax.ShapeDtypeStruct((span, half), jnp.bfloat16),
            jax.ShapeDtypeStruct((span, half // 2), jnp.bfloat16),
        ],
        compiler_params=pltpu.CompilerParams(vmem_limit_bytes=16 << 20),
        name="norm",
    )(scalars, mine, other, gain)


def slots(scalars_ref, table_ref, plane, share):
    core, layer = scalars_ref[1], scalars_ref[2]
    span = table_ref.shape[1]
    ids = lax.broadcasted_iota(jnp.int32, (plane, span), 0) * RING + layer
    ids = ids.astype(jnp.float32)
    member = jnp.zeros((plane, span), jnp.float32)
    weight = jnp.zeros((plane, span), jnp.float32)
    for k in range(TOP):
        hit = table_ref[k : k + 1, :] == ids
        member = jnp.where(hit, 1.0, member)
        weight = jnp.where(hit, table_ref[TOP + k : TOP + k + 1, :], weight)
    earlier = lax.broadcasted_iota(jnp.int32, (span, span), 0) < lax.broadcasted_iota(
        jnp.int32, (span, span), 1
    )
    rank = jnp.dot(
        member.astype(jnp.bfloat16),
        earlier.astype(jnp.float32).astype(jnp.bfloat16),
        preferred_element_type=jnp.float32,
    )
    slot = jnp.where(member > 0.0, rank - (core * share).astype(jnp.float32), -1.0)
    shape = (plane, share, span)
    wanted = lax.broadcasted_iota(jnp.int32, shape, 1).astype(jnp.float32)
    chosen = jnp.broadcast_to(slot[:, None, :], shape) == wanted
    return chosen, weight


def dispatch_kernel(plane, share, scalars_ref, *refs):
    count = (len(refs) - 1) // 3
    out_ref = refs[-1]
    core = scalars_ref[1]
    for r in range(count):
        table_ref, mine_ref, other_ref = refs[3 * r : 3 * r + 3]
        half = mine_ref.shape[1]
        chosen, _ = slots(scalars_ref, table_ref, plane, share)
        select = jnp.where(chosen, 1.0, 0.0).reshape(plane * share, chosen.shape[2])
        select = select.astype(jnp.bfloat16)
        for ref, which in ((mine_ref, core), (other_ref, 1 - core)):
            rows = jnp.dot(select, ref[...], preferred_element_type=jnp.float32)
            rows = rows.astype(jnp.bfloat16).reshape(plane, share, half)
            out_ref[:, r * share : (r + 1) * share, lanes(which * half, half)] = rows


def dispatch(scalars, plane, share, items):
    count = len(items)
    half = items[0][1].shape[1]
    return pl.pallas_call(
        lambda *refs: dispatch_kernel(plane, share, *refs),
        in_specs=[SMEM] + [VMEM] * (3 * count),
        out_specs=VMEM,
        out_shape=jax.ShapeDtypeStruct((plane, count * share, 2 * half), jnp.bfloat16),
        compiler_params=pltpu.CompilerParams(vmem_limit_bytes=24 << 20),
        name="dispatch",
    )(scalars, *[part for item in items for part in item])


def combine_kernel(kind, count, plane, share, scalars_ref, *refs):
    tables, rows_ref = refs[:count], refs[count]
    keep_ref, pass_ref, send_ref = refs[count + 1 :]
    chip, core = scalars_ref[0], scalars_ref[1]
    quarter = rows_ref.shape[2] // 4

    def mixer(table, r):
        chosen, weight = slots(scalars_ref, table, plane, share)
        high = weight.astype(jnp.bfloat16).astype(jnp.float32)
        mixes = []
        for w in (high, weight - high):
            mix = jnp.where(chosen, jnp.broadcast_to(w[:, None, :], chosen.shape), 0.0)
            mixes.append(mix.reshape(plane * share, chosen.shape[2]).astype(jnp.bfloat16))

        def mixture(its_chip, its_core):
            start = pl.multiple_of(r * share, share)
            columns = lanes((2 * its_chip + its_core) * quarter, quarter)
            rows = rows_ref[:, pl.ds(start, share), columns].reshape(plane * share, quarter)
            return sum(
                lax.dot_general(mix, rows, TN, preferred_element_type=jnp.float32) for mix in mixes
            )

        return mixture

    if kind == "pair":
        down, up = tables[0][...], tables[1][...]
        here = jnp.where(chip == 1, 1, 0)
        keeper = mixer(jnp.where(chip == 1, up, down), here)
        passer = mixer(jnp.where(chip == 1, down, up), 1 - here)
        parts = [(keeper, 0), (keeper, 1), (passer, 0), (passer, 1)]
    else:
        only = mixer(tables[0][...], 0)
        parts = [(only, chip), (only, 1 - chip)] if kind == "own" else [(only, 1 - chip), (only, chip)]
    each = len(parts) // 2
    for i, (mixture, its_chip) in enumerate(parts):
        out_ref = keep_ref if i < each else pass_ref
        place = i % each * quarter
        out_ref[:, place : place + quarter] = mixture(its_chip, core)
        sent = mixture(its_chip, 1 - core)
        send_ref[:, i * quarter : (i + 1) * quarter] = sent.astype(jnp.bfloat16)


def combine(kind, scalars, plane, share, tables, rows):
    span = tables[0].shape[1]
    width = rows.shape[2] // 4 * (2 if kind == "pair" else 1)
    count = len(tables)
    return pl.pallas_call(
        lambda *refs: combine_kernel(kind, count, plane, share, *refs),
        in_specs=[SMEM] + [VMEM] * (count + 1),
        out_specs=[VMEM] * 3,
        out_shape=[
            jax.ShapeDtypeStruct((span, width), jnp.float32),
            jax.ShapeDtypeStruct((span, width), jnp.float32),
            jax.ShapeDtypeStruct((span, 2 * width), jnp.bfloat16),
        ],
        compiler_params=pltpu.CompilerParams(vmem_limit_bytes=24 << 20),
        name="combine",
    )(scalars, *tables, rows)


def close_kernel(scalars_ref, keep_ref, onward_ref, came_ref, home_ref, keep_out, onward_out):
    chip = scalars_ref[0]
    quarter = keep_ref.shape[1]
    mine = home_ref[:, lanes(chip * quarter, quarter)].astype(jnp.float32)
    other = home_ref[:, lanes((1 - chip) * quarter, quarter)].astype(jnp.float32)
    keep_out[...] = keep_ref[...] + came_ref[:, :quarter].astype(jnp.float32) + mine
    onward = onward_ref[...] + came_ref[:, quarter:].astype(jnp.float32) + other
    onward_out[...] = onward.astype(jnp.bfloat16)


def close(scalars, keep, onward, came, home):
    return pl.pallas_call(
        close_kernel,
        in_specs=[SMEM] + [VMEM] * 4,
        out_specs=[VMEM] * 2,
        out_shape=[
            jax.ShapeDtypeStruct(keep.shape, jnp.float32),
            jax.ShapeDtypeStruct(onward.shape, jnp.bfloat16),
        ],
        compiler_params=pltpu.CompilerParams(vmem_limit_bytes=8 << 20),
        name="close",
    )(scalars, keep, onward, came, home)


def fold_kernel(keep_ref, onward_ref, came_ref, keep_out, onward_out):
    quarter = keep_ref.shape[1]
    keep_out[...] = keep_ref[...] + came_ref[:, :quarter].astype(jnp.float32)
    onward = onward_ref[...] + came_ref[:, quarter:].astype(jnp.float32)
    onward_out[...] = onward.astype(jnp.bfloat16)


def fold(keep, onward, came):
    return pl.pallas_call(
        fold_kernel,
        in_specs=[VMEM] * 3,
        out_specs=[VMEM] * 2,
        out_shape=[
            jax.ShapeDtypeStruct(keep.shape, jnp.float32),
            jax.ShapeDtypeStruct(onward.shape, jnp.bfloat16),
        ],
        compiler_params=pltpu.CompilerParams(vmem_limit_bytes=8 << 20),
        name="fold",
    )(keep, onward, came)


def total_kernel(keep_ref, came_ref, out_ref):
    out_ref[...] = (keep_ref[...] + came_ref[...].astype(jnp.float32)).astype(jnp.bfloat16)


def total_of(keep, came):
    return pl.pallas_call(
        total_kernel,
        in_specs=[VMEM] * 2,
        out_specs=VMEM,
        out_shape=jax.ShapeDtypeStruct(keep.shape, jnp.bfloat16),
        compiler_params=pltpu.CompilerParams(vmem_limit_bytes=8 << 20),
        name="total",
    )(keep, came)


def expert_kernel(slices, x_ref, *refs):
    weights = refs[: 3 * slices]
    out_ref, held, total, sems = refs[3 * slices :]
    block = total.shape[0]
    copies = [
        pltpu.make_async_copy(weights[i], held.at[i], sems.at[i]) for i in range(3 * slices)
    ]
    for copy in copies:
        copy.start()

    def step(i, carry):
        number, j = i // slices, i % slices
        start = pl.multiple_of(number * block, block)

        def arrive(k):
            @pl.when(number == 0)
            def _():
                pltpu.make_async_copy(weights[k], held.at[3 * j + k], sems.at[3 * j + k]).wait()

        x = x_ref[pl.ds(start, block), :]
        arrive(0)
        gate = lax.dot_general(x, held[3 * j], NT, preferred_element_type=jnp.float32)
        arrive(1)
        upper = lax.dot_general(x, held[3 * j + 1], NT, preferred_element_type=jnp.float32)
        act = (gate / (1.0 + jnp.exp(-gate)) * upper).astype(jnp.bfloat16)
        arrive(2)
        part = jnp.dot(act, held[3 * j + 2], preferred_element_type=jnp.float32)

        @pl.when(j == 0)
        def _():
            total[...] = part

        @pl.when((j > 0) & (j < slices - 1))
        def _():
            total[...] += part

        @pl.when(j == slices - 1)
        def _():
            out_ref[pl.ds(start, block), :] = (total[...] + part).astype(jnp.bfloat16)

        return carry

    lax.fori_loop(0, x_ref.shape[0] // block * slices, step, 0)


def expert(inbox, weights):
    rows, width = inbox.shape[0] * inbox.shape[1], inbox.shape[2]
    units = weights[0].shape[0]
    count = len(weights)
    block = min(rows, 256)
    out = pl.pallas_call(
        lambda *refs: expert_kernel(count // 3, *refs),
        in_specs=[VMEM] + [pl.BlockSpec(memory_space=pl.ANY)] * count,
        out_specs=VMEM,
        out_shape=jax.ShapeDtypeStruct((rows, width), jnp.bfloat16),
        scratch_shapes=[
            pltpu.VMEM((count, units, width), jnp.bfloat16),
            pltpu.VMEM((block, width), jnp.float32),
            pltpu.SemaphoreType.DMA((count,)),
        ],
        cost_estimate=pl.CostEstimate(
            flops=2 * count * rows * width * units,
            transcendentals=rows * units * count // 3,
            bytes_accessed=2 * count * units * width + 4 * rows * width,
        ),
        name="expert",
    )(inbox.reshape(rows, width), *weights)
    return out.reshape(inbox.shape)


def stage_kernel(scalars_ref, k_ref, v_ref, ck_ref, cv_ref, *outs):
    me, length = scalars_ref[0], scalars_ref[1]
    block = k_ref.shape[0]
    last = ck_ref.shape[0] // block - 1
    for mask, out_ref in enumerate(outs):
        peer = me ^ mask
        start = pl.multiple_of(jnp.minimum(peer, last) * block, block)
        row = lax.broadcasted_iota(jnp.int32, (block, block), 0) + peer * block - length
        moved = row == lax.broadcasted_iota(jnp.int32, (block, block), 1)
        moved = jnp.where(moved, 1.0, 0.0).astype(jnp.bfloat16)
        for which, (fresh_ref, cached_ref) in enumerate(((k_ref, ck_ref), (v_ref, cv_ref))):
            fresh = jnp.dot(moved, fresh_ref[...], preferred_element_type=jnp.float32)
            kept = cached_ref[pl.ds(start, block), :].astype(jnp.float32)
            old = lax.broadcasted_iota(jnp.int32, kept.shape, 0) + peer * block < length
            out_ref[which] = jnp.where(old, kept, fresh).astype(jnp.bfloat16)


def stage(scalars, span_k, span_v, cache_k, cache_v, pieces):
    span, columns = span_k.shape
    return pl.pallas_call(
        stage_kernel,
        in_specs=[SMEM] + [VMEM] * 4,
        out_specs=[VMEM] * pieces,
        out_shape=[jax.ShapeDtypeStruct((2, span, columns), jnp.bfloat16)] * pieces,
        compiler_params=pltpu.CompilerParams(vmem_limit_bytes=32 << 20),
        name="stage",
    )(scalars, span_k, span_v, cache_k, cache_v)


def join_kernel(scalars_ref, *refs):
    out_ref = refs[-1]
    columns = refs[0].shape[2]
    for mask, ref in enumerate(refs[:-1]):
        out_ref[:, :, lanes((scalars_ref[0] ^ mask) * columns, columns)] = ref[...]


def join(scalars, pieces):
    kinds, block, columns = pieces[0].shape
    return pl.pallas_call(
        join_kernel,
        in_specs=[SMEM] + [VMEM] * len(pieces),
        out_specs=VMEM,
        out_shape=jax.ShapeDtypeStruct((kinds, block, columns * len(pieces)), jnp.bfloat16),
        compiler_params=pltpu.CompilerParams(vmem_limit_bytes=16 << 20),
        name="join",
    )(scalars, *pieces)


def flip(value, mask):
    groups = lax.axis_size("tensor")
    return lax.ppermute(value, "tensor", [(i, i ^ mask) for i in range(groups)])


def along(value, step):
    count = lax.axis_size("request")
    pairs = [(i, i // RING * RING + (i + step) % RING) for i in range(count)]
    return lax.ppermute(value, "request", pairs)


def homeward(value, gap):
    count, groups = lax.axis_size("request"), lax.axis_size("tensor")
    pairs = []
    for i in range(count):
        for t in range(groups):
            to = (i + (gap if t // 2 else -gap)) % RING + i // RING * RING
            pairs.append((t * count + i, (t ^ 2) * count + to))
    return lax.ppermute(value, ("tensor", "request"), pairs)


def on_device(
    hidden_in,
    span_q,
    span_k,
    span_v,
    cache_k,
    cache_v,
    cached_len,
    out_proj,
    norm_gain,
    routes,
    route_weight,
    w_gate,
    w_up,
    w_down,
):
    span, width = hidden_in.shape
    groups = lax.axis_size("tensor")
    experts = lax.axis_size("request")
    plane = experts // RING
    half = width // 2
    me = lax.axis_index("tensor")
    core = me % 2
    chip = me // 2
    layer = lax.axis_index("request") % RING
    length = cached_len[0]
    planes = [[column * RING + z for column in range(plane)] for z in range(RING)]
    scalars = jnp.stack([chip, core, layer]).astype(jnp.int32)

    def exchange(value):
        return lax.all_to_all(
            value, "request", split_axis=0, concat_axis=0, axis_index_groups=planes, tiled=True
        )

    own_w = (jnp.swapaxes(w_gate[0], 0, 1), jnp.swapaxes(w_up[0], 0, 1), w_down[0])
    near_w = tuple(flip(w, 1) for w in own_w)
    weights = own_w + near_w

    most = max(2, 2 * span * TOP // experts)
    share = most // 2
    table = jnp.concatenate([routes.T.astype(jnp.float32), route_weight.T], axis=0)
    tables = {0: table}
    for step in (1, -1, 2):
        tables[step] = along(table, step)

    keep, send = attend(
        jnp.stack([length, core]).astype(jnp.int32),
        span_q,
        span_k,
        span_v,
        cache_k[0],
        cache_v[0],
        out_proj,
    )
    keep = keep + flip(send, 1).astype(jnp.float32)
    keep = keep + flip(keep.astype(jnp.bfloat16), 2).astype(jnp.float32)
    hidden_half = lax.dynamic_slice_in_dim(hidden_in, core * half, half, 1)
    mixed_half = (hidden_half.astype(jnp.float32) + keep).astype(jnp.bfloat16)
    mine, other, own_mixed = norm(
        scalars, mixed_half, flip(mixed_half, 1), norm_gain.reshape(1, width)
    )

    tokens = {0: (mine, other)}
    for step in (1, -1, 2):
        came = along(mine, step)
        tokens[step] = (came, flip(came, 1))

    chunks = ((0,), (1, -1), (2,))
    outs = []
    for steps in chunks:
        outbox = dispatch(scalars, plane, share, [(tables[step],) + tokens[step] for step in steps])
        inbox = exchange(outbox)
        outs.append(expert(inbox, weights))

    def gather(kind, number, steps):
        returned = exchange(outs[number])
        keep, onward, send = combine(
            kind, scalars, plane, share, [tables[step] for step in steps], returned
        )
        return keep, onward, flip(send, 1)

    homes = []
    for kind, number, gap in (("pair", 1, 1), ("far", 2, 2)):
        keep, onward, came = gather(kind, number, chunks[number])
        keep, onward = fold(keep, onward, came)
        came = flip(onward, 2)
        keep = total_of(keep, came)
        homes.append(homeward(keep, gap))
    keep, onward, came = gather("own", 0, chunks[0])
    keep, onward = close(scalars, keep, onward, came, homes[0])
    came = flip(onward, 2)
    result = own_mixed.astype(jnp.float32) + keep
    result = result + came.astype(jnp.float32) + homes[1].astype(jnp.float32)
    layer_out = result.astype(jnp.bfloat16)

    spot = jnp.stack([me, length]).astype(jnp.int32)
    pieces = stage(spot, span_k, span_v, cache_k[0], cache_v[0], groups)
    pieces = [pieces[0]] + [flip(pieces[m], m) for m in range(1, groups)]
    decode = join(spot, pieces)
    return (layer_out, decode[None])


def solution(mesh):
    in_specs = (
        P("request", None),
        P("request", "tensor"),
        P("request", "tensor"),
        P("request", "tensor"),
        P("request", None, "tensor"),
        P("request", None, "tensor"),
        P("request"),
        P("tensor", None),
        P(),
        P("request", None),
        P("request", None),
        P("request", None, "tensor"),
        P("request", None, "tensor"),
        P("request", "tensor", None),
    )
    out_specs = (P("request", "tensor"), P("request", None, "tensor", None))

    return jax.shard_map(
        on_device, mesh=mesh, in_specs=in_specs, out_specs=out_specs, check_vma=False
    )
```

profile of v0, /device:TPU:32, one launch (start us, length us, event | category | flops | bytes accessed | tf_op | source)
XLA Modules:
  0.0 267.7 jit_solution(10596273308617134164)
XLA Ops:
  1.9 8.5 %attend.1 = (f32[256,1024]{1,0:T(8,128)}, bf16[256,1024]{1,0:T(8,128)(2,1)}) custom-call(s32[2]{0:T(128)} %pad_add_fusion.1.scalars_ref, bf16[256,512]{1,0:T(8,128)(2,1)} %q_ref.1, bf16[256,512]{1,0:T(8,128)(2,1)} %k_ref.3, bf16[256,512]{1,0:T(8,128)(2,1)} %v_ref.3, bf16[768,512]{1,0:T(8,128)(2,1)} %bitcast.24, bf16[768,512]{1,0:T(8,128)(2,1)} %bitcast.26, ...), custom_call_target="tpu_custom_call" | custom-call | flops 1073741824 | bytes 9437184 | tf_op jit(solution)/shard_map/attend/pallas_call | solution.py:78
  15.8 12.2 %collective-permute-done.1 = bf16[256,1024]{1,0:T(8,128)(2,1)S(1)} collective-permute-done((bf16[256,1024]{1,0:T(8,128)(2,1)S(1)}, bf16[256,1024]{1,0:T(8,128)(2,1)S(1)}, u32[]{:S(2)}, u32[]{:S(2)}) %collective-permute-start.1) | collective-permute-done | bytes 524320 | tf_op jit(solution)/shard_map/ppermute | solution.py:442
  32.4 5.4 %collective-permute-start.11 = (bf16[256,1024]{1,0:T(8,128)(2,1)S(1)}, bf16[256,1024]{1,0:T(8,128)(2,1)S(1)}, u32[]{:S(2)}, u32[]{:S(2)}) collective-permute-start(bf16[256,1024]{1,0:T(8,128)(2,1)S(1)} %get-tuple-element.29.refs_2_), channel_id=1, source_target_pairs={{0,3},{1,0},{2,1},{3,2},{4,7},{5,4},{6,5},{7,6},{8,11},{9,8},{10,9... | collective-permute-start | bytes 1572872 | tf_op jit(solution)/shard_map/ppermute | solution.py:448
  40.0 7.1 %all-to-all-start = ((bf16[16,16,2048]{2,1,0:T(8,128)(2,1)}), bf16[16,16,2048]{2,1,0:T(8,128)(2,1)}, u32[]{:S(2)}, u32[]{:S(2)}) async-start(bf16[16,16,2048]{2,1,0:T(8,128)(2,1)} %dispatch.3), calls=%async_computation | async-start | bytes 2097152 | tf_op jit(solution)/shard_map/all_to_all | solution.py:491
  47.0 13.1 %collective-permute-done.11.refs_5_ = bf16[256,1024]{1,0:T(8,128)(2,1)S(1)} collective-permute-done((bf16[256,1024]{1,0:T(8,128)(2,1)S(1)}, bf16[256,1024]{1,0:T(8,128)(2,1)S(1)}, u32[]{:S(2)}, u32[]{:S(2)}) %collective-permute-start.11) | collective-permute-done | bytes 524320 | tf_op jit(solution)/shard_map/ppermute | solution.py:448
  60.1 4.7 %collective-permute-done.9.refs_2_ = bf16[256,1024]{1,0:T(8,128)(2,1)S(1)} collective-permute-done((bf16[256,1024]{1,0:T(8,128)(2,1)S(1)}, bf16[256,1024]{1,0:T(8,128)(2,1)S(1)}, u32[]{:S(2)}, u32[]{:S(2)}) %collective-permute-start.9) | collective-permute-done | bytes 524320 | tf_op jit(solution)/shard_map/ppermute | solution.py:448
  65.2 2.5 collective-permute-start.7
  71.0 2.8 %dispatch.4 = bf16[16,32,2048]{2,1,0:T(8,128)(2,1)} custom-call(s32[3]{0:T(128)S(1)} %pad_add_fusion.scalars_ref.refs_0_, f32[8,256]{1,0:T(8,128)S(1)} %collective-permute-done.7.refs_1_, bf16[256,1024]{1,0:T(8,128)(2,1)S(1)} %collective-permute-done.9.refs_2_, bf16[256,1024]{1,0:T(8,128)(2,1)S(1)} %collective-permute-done.10.refs_3_, ...), custom_call_target="tpu_custom_call" | custom-call | tf_op jit(solution)/shard_map/dispatch/pallas_call | solution.py:192
  73.8 7.1 %all-to-all-start.2 = ((bf16[16,32,2048]{2,1,0:T(8,128)(2,1)}), bf16[16,32,2048]{2,1,0:T(8,128)(2,1)}, u32[]{:S(2)}, u32[]{:S(2)}) async-start(bf16[16,32,2048]{2,1,0:T(8,128)(2,1)} %dispatch.4), calls=%async_computation.2 | async-start | bytes 4194304 | tf_op jit(solution)/shard_map/all_to_all | solution.py:491
  81.0 2.4 collective-permute-start.18
  83.9 25.1 %collective-permute-done.18.refs_2_ = bf16[256,1024]{1,0:T(8,128)(2,1)S(1)} collective-permute-done((bf16[256,1024]{1,0:T(8,128)(2,1)S(1)}, bf16[256,1024]{1,0:T(8,128)(2,1)S(1)}, u32[]{:S(2)}, u32[]{:S(2)}) %collective-permute-start.18) | collective-permute-done | bytes 524320 | tf_op jit(solution)/shard_map/ppermute | solution.py:448
  109.0 2.4 collective-permute-start.17
  111.3 5.2 %collective-permute-done.17.refs_1_ = f32[8,256]{1,0:T(8,128)S(1)} collective-permute-done((f32[8,256]{1,0:T(8,128)S(1)}, f32[8,256]{1,0:T(8,128)S(1)}, u32[]{:S(2)}, u32[]{:S(2)}) %collective-permute-start.17) | collective-permute-done | bytes 8224 | tf_op jit(solution)/shard_map/ppermute | solution.py:448
  116.5 2.2 dispatch.5
  118.7 6.8 %all-to-all-start.4 = ((bf16[16,16,2048]{2,1,0:T(8,128)(2,1)}), bf16[16,16,2048]{2,1,0:T(8,128)(2,1)S(1)}, u32[]{:S(2)}, u32[]{:S(2)}) async-start(bf16[16,16,2048]{2,1,0:T(8,128)(2,1)} %dispatch.5), calls=%async_computation.4 | async-start | bytes 2097152 | tf_op jit(solution)/shard_map/all_to_all | solution.py:491
  125.6 13.9 %expert.4 = bf16[512,2048]{1,0:T(8,128)(2,1)} custom-call(bf16[512,2048]{1,0:T(8,128)(2,1)} %bitcast.17.refs_0_, bf16[352,2048]{1,0:T(8,128)(2,1)} %bitcast.29, bf16[352,2048]{1,0:T(8,128)(2,1)} %bitcast.34, bf16[352,2048]{1,0:T(8,128)(2,1)} %bitcast.38, bf16[352,2048]{1,0:T(8,128)(2,1)} %collective-permute-done.3.refs_4_, ...), custom_call_target="tpu_custom_call" | custom-call | flops 4429185024 | bytes 12845056 | tf_op jit(solution)/shard_map/expert/pallas_call | solution.py:372
  139.5 3.1 %all-to-all-done.4 = bf16[16,16,2048]{2,1,0:T(8,128)(2,1)S(1)} async-done(((bf16[16,16,2048]{2,1,0:T(8,128)(2,1)}), bf16[16,16,2048]{2,1,0:T(8,128)(2,1)S(1)}, u32[]{:S(2)}, u32[]{:S(2)}) %all-to-all-start.4) | async-done | bytes 1048608 | tf_op jit(solution)/shard_map/all_to_all | solution.py:491
  143.6 4.1 %all-to-all-start.3 = ((bf16[16,32,2048]{2,1,0:T(8,128)(2,1)}), bf16[16,32,2048]{2,1,0:T(8,128)(2,1)S(1)}, u32[]{:S(2)}, u32[]{:S(2)}) async-start(bf16[16,32,2048]{2,1,0:T(8,128)(2,1)} %bitcast.45), calls=%async_computation.3 | async-start | bytes 4194304 | tf_op jit(solution)/shard_map/all_to_all | solution.py:491
  147.8 8.4 %expert.5 = bf16[256,2048]{1,0:T(8,128)(2,1)} custom-call(bf16[256,2048]{1,0:T(8,128)(2,1)} %bitcast.43, bf16[352,2048]{1,0:T(8,128)(2,1)} %bitcast.30, bf16[352,2048]{1,0:T(8,128)(2,1)} %bitcast.35, bf16[352,2048]{1,0:T(8,128)(2,1)} %bitcast.39, bf16[352,2048]{1,0:T(8,128)(2,1)} %collective-permute-done.3.refs_4_, ...), custom_call_target="tpu_custom_call" | custom-call | flops 2214592512 | bytes 10747904 | tf_op jit(solution)/shard_map/expert/pallas_call | solution.py:372
  156.1 20.3 %all-to-all-done.3.refs_3_ = bf16[16,32,2048]{2,1,0:T(8,128)(2,1)S(1)} async-done(((bf16[16,32,2048]{2,1,0:T(8,128)(2,1)}), bf16[16,32,2048]{2,1,0:T(8,128)(2,1)S(1)}, u32[]{:S(2)}, u32[]{:S(2)}) %all-to-all-start.3) | async-done | bytes 2097184 | tf_op jit(solution)/shard_map/all_to_all | solution.py:491
  176.5 3.7 %all-to-all-start.5 = ((bf16[16,16,2048]{2,1,0:T(8,128)(2,1)}), bf16[16,16,2048]{2,1,0:T(8,128)(2,1)S(1)}, u32[]{:S(2)}, u32[]{:S(2)}) async-start(bf16[16,16,2048]{2,1,0:T(8,128)(2,1)} %bitcast.42), calls=%async_computation.5 | async-start | bytes 2097152 | tf_op jit(solution)/shard_map/all_to_all | solution.py:491
  180.2 3.0 %combine.4 = (f32[256,1024]{1,0:T(8,128)S(1)}, f32[256,1024]{1,0:T(8,128)S(1)}, bf16[256,2048]{1,0:T(8,128)(2,1)}) custom-call(s32[3]{0:T(128)S(1)} %pad_add_fusion.scalars_ref.refs_0_, f32[8,256]{1,0:T(8,128)S(1)} %collective-permute-done.7.refs_1_, f32[8,256]{1,0:T(8,128)S(1)} %collective-permute-done.8.refs_4_.refs_2_, ...), custom_call_target="tpu_custom_call" | custom-call | tf_op jit(solution)/shard_map/combine/pallas_call | solution.py:248
  185.2 8.4 %expert.3 = bf16[256,2048]{1,0:T(8,128)(2,1)} custom-call(bf16[256,2048]{1,0:T(8,128)(2,1)} %bitcast.8.refs_0_, bf16[352,2048]{1,0:T(8,128)(2,1)} %bitcast.31, bf16[352,2048]{1,0:T(8,128)(2,1)} %bitcast.36, bf16[352,2048]{1,0:T(8,128)(2,1)} %bitcast.40, bf16[352,2048]{1,0:T(8,128)(2,1)} %collective-permute-done.3.refs_4_, ...), custom_call_target="tpu_custom_call" | custom-call | flops 2214592512 | bytes 10747904 | tf_op jit(solution)/shard_map/expert/pallas_call | solution.py:372
  195.0 6.0 %all-to-all-start.1 = ((bf16[16,16,2048]{2,1,0:T(8,128)(2,1)}), bf16[16,16,2048]{2,1,0:T(8,128)(2,1)S(1)}, u32[]{:S(2)}, u32[]{:S(2)}) async-start(bf16[16,16,2048]{2,1,0:T(8,128)(2,1)} %bitcast.41), calls=%async_computation.1 | async-start | bytes 2097152 | tf_op jit(solution)/shard_map/all_to_all | solution.py:491
  201.0 2.3 combine.5
  204.9 2.2 fold.2
  207.8 11.7 %all-to-all-done.1.refs_2_ = bf16[16,16,2048]{2,1,0:T(8,128)(2,1)S(1)} async-done(((bf16[16,16,2048]{2,1,0:T(8,128)(2,1)}), bf16[16,16,2048]{2,1,0:T(8,128)(2,1)S(1)}, u32[]{:S(2)}, u32[]{:S(2)}) %all-to-all-start.1) | async-done | bytes 1048608 | tf_op jit(solution)/shard_map/all_to_all | solution.py:491
  229.4 4.3 %collective-permute-done.21.came_ref = bf16[256,512]{1,0:T(8,128)(2,1)S(1)} collective-permute-done((bf16[256,512]{1,0:T(8,128)(2,1)S(1)}, bf16[256,512]{1,0:T(8,128)(2,1)S(1)}, u32[]{:S(2)}, u32[]{:S(2)}) %collective-permute-start.21) | collective-permute-done | bytes 262176 | tf_op jit(solution)/shard_map/ppermute | solution.py:442
  235.3 6.6 %collective-permute-done.15.home_ref = bf16[256,1024]{1,0:T(8,128)(2,1)S(1)} collective-permute-done((bf16[256,1024]{1,0:T(8,128)(2,1)S(1)}, bf16[256,1024]{1,0:T(8,128)(2,1)S(1)}, u32[]{:S(2)}, u32[]{:S(2)}) %collective-permute-start.15) | collective-permute-done | bytes 524320 | tf_op jit(solution)/shard_map/ppermute | solution.py:458
  242.7 7.6 %collective-permute-start.16 = (bf16[256,512]{1,0:T(8,128)(2,1)S(1)}, bf16[256,512]{1,0:T(8,128)(2,1)S(1)}, u32[]{:S(2)}, u32[]{:S(2)}) collective-permute-start(bf16[256,512]{1,0:T(8,128)(2,1)S(1)} %get-tuple-element.40), channel_id=1, source_target_pairs={{0,128},{64,192},{128,0},{192,64},{1,129},{65,193},{129,1},{193,65... | collective-permute-start | bytes 786440 | tf_op jit(solution)/shard_map/ppermute | solution.py:442
  250.3 10.4 %collective-permute-done.25.refs_3_ = bf16[2,256,512]{2,1,0:T(8,128)(2,1)S(1)} collective-permute-done((bf16[2,256,512]{2,1,0:T(8,128)(2,1)S(1)}, bf16[2,256,512]{2,1,0:T(8,128)(2,1)S(1)}, u32[]{:S(2)}, u32[]{:S(2)}) %collective-permute-start.25) | collective-permute-done | bytes 524320 | tf_op jit(solution)/shard_map/ppermute | solution.py:442
  262.6 4.2 %collective-permute-done.16 = bf16[256,512]{1,0:T(8,128)(2,1)S(1)} collective-permute-done((bf16[256,512]{1,0:T(8,128)(2,1)S(1)}, bf16[256,512]{1,0:T(8,128)(2,1)S(1)}, u32[]{:S(2)}, u32[]{:S(2)}) %collective-permute-start.16) | collective-permute-done | bytes 262176 | tf_op jit(solution)/shard_map/ppermute | solution.py:442
  (94 shorter events, 38.4 us)
Async XLA Ops:
  10.4 2.1 collective-permute-start
  13.9 14.1 %collective-permute-start.1 = (bf16[256,1024]{1,0:T(8,128)(2,1)S(1)}, bf16[256,1024]{1,0:T(8,128)(2,1)S(1)}, u32[]{:S(2)}, u32[]{:S(2)}) collective-permute-start(bf16[256,1024]{1,0:T(8,128)(2,1)S(1)} %fusion), channel_id=1, source_target_pairs={{0,128},{64,192},{128,0},{192,64},{1,129},{65,193},{129,1},{193,65... | collective-permute-start | bytes 1572872 | tf_op jit(solution)/shard_map/ppermute | solution.py:442
  29.4 2.0 collective-permute-start.2
  32.4 27.7 %collective-permute-start.11 = (bf16[256,1024]{1,0:T(8,128)(2,1)S(1)}, bf16[256,1024]{1,0:T(8,128)(2,1)S(1)}, u32[]{:S(2)}, u32[]{:S(2)}) collective-permute-start(bf16[256,1024]{1,0:T(8,128)(2,1)S(1)} %get-tuple-element.29.refs_2_), channel_id=1, source_target_pairs={{0,3},{1,0},{2,1},{3,2},{4,7},{5,4},{6,5},{7,6},{8,11},{9,8},{10,9... | collective-permute-start | bytes 1572872 | tf_op jit(solution)/shard_map/ppermute | solution.py:448
  37.8 27.0 %collective-permute-start.9 = (bf16[256,1024]{1,0:T(8,128)(2,1)S(1)}, bf16[256,1024]{1,0:T(8,128)(2,1)S(1)}, u32[]{:S(2)}, u32[]{:S(2)}) collective-permute-start(bf16[256,1024]{1,0:T(8,128)(2,1)S(1)} %get-tuple-element.29.refs_2_), channel_id=1, source_target_pairs={{0,1},{1,2},{2,3},{3,0},{4,5},{5,6},{6,7},{7,4},{8,9},{9,10},{10,1... | collective-permute-start | bytes 1572872 | tf_op jit(solution)/shard_map/ppermute | solution.py:448
  40.0 33.9 %all-to-all-start = ((bf16[16,16,2048]{2,1,0:T(8,128)(2,1)}), bf16[16,16,2048]{2,1,0:T(8,128)(2,1)}, u32[]{:S(2)}, u32[]{:S(2)}) async-start(bf16[16,16,2048]{2,1,0:T(8,128)(2,1)} %dispatch.3), calls=%async_computation | async-start | bytes 2097152 | tf_op jit(solution)/shard_map/all_to_all | solution.py:491
  60.1 10.9 %collective-permute-start.12 = (bf16[256,1024]{1,0:T(8,128)(2,1)S(1)}, bf16[256,1024]{1,0:T(8,128)(2,1)S(1)}, u32[]{:S(2)}, u32[]{:S(2)}) collective-permute-start(bf16[256,1024]{1,0:T(8,128)(2,1)S(1)} %collective-permute-done.11.refs_5_), channel_id=1, source_target_pairs={{0,64},{64,0},{128,192},{192,128},{1,65},{65,1},{129,193},{193,129... | collective-permute-start | bytes 1572872 | tf_op jit(solution)/shard_map/ppermute | solution.py:442
  64.8 6.2 %collective-permute-start.10 = (bf16[256,1024]{1,0:T(8,128)(2,1)S(1)}, bf16[256,1024]{1,0:T(8,128)(2,1)S(1)}, u32[]{:S(2)}, u32[]{:S(2)}) collective-permute-start(bf16[256,1024]{1,0:T(8,128)(2,1)S(1)} %collective-permute-done.9.refs_2_), channel_id=1, source_target_pairs={{0,64},{64,0},{128,192},{192,128},{1,65},{65,1},{129,193},{193,129... | collective-permute-start | bytes 1572872 | tf_op jit(solution)/shard_map/ppermute | solution.py:442
  64.8 4.6 %collective-permute-start.8 = (f32[8,256]{1,0:T(8,128)S(1)}, f32[8,256]{1,0:T(8,128)S(1)}, u32[]{:S(2)}, u32[]{:S(2)}) collective-permute-start(f32[8,256]{1,0:T(8,128)S(1)} %pad_maximum_fusion.refs_1_), channel_id=1, source_target_pairs={{0,3},{1,0},{2,1},{3,2},{4,7},{5,4},{6,5},{7,6},{8,11},{9,8},{10,9... | collective-permute-start | bytes 24584 | tf_op jit(solution)/shard_map/ppermute | solution.py:448
  65.2 5.8 %collective-permute-start.7 = (f32[8,256]{1,0:T(8,128)S(1)}, f32[8,256]{1,0:T(8,128)S(1)}, u32[]{:S(2)}, u32[]{:S(2)}) collective-permute-start(f32[8,256]{1,0:T(8,128)S(1)} %pad_maximum_fusion.refs_1_), channel_id=1, source_target_pairs={{0,1},{1,2},{2,3},{3,0},{4,5},{5,6},{6,7},{7,4},{8,9},{9,10},{10,1... | collective-permute-start | bytes 24584 | tf_op jit(solution)/shard_map/ppermute | solution.py:448
  73.8 44.9 %all-to-all-start.2 = ((bf16[16,32,2048]{2,1,0:T(8,128)(2,1)}), bf16[16,32,2048]{2,1,0:T(8,128)(2,1)}, u32[]{:S(2)}, u32[]{:S(2)}) async-start(bf16[16,32,2048]{2,1,0:T(8,128)(2,1)} %dispatch.4), calls=%async_computation.2 | async-start | bytes 4194304 | tf_op jit(solution)/shard_map/all_to_all | solution.py:491
  81.0 28.0 %collective-permute-start.18 = (bf16[256,1024]{1,0:T(8,128)(2,1)S(1)}, bf16[256,1024]{1,0:T(8,128)(2,1)S(1)}, u32[]{:S(2)}, u32[]{:S(2)}) collective-permute-start(bf16[256,1024]{1,0:T(8,128)(2,1)S(1)} %get-tuple-element.29.refs_2_), channel_id=1, source_target_pairs={{0,2},{1,3},{2,0},{3,1},{4,6},{5,7},{6,4},{7,5},{8,10},{9,11},{10,... | collective-permute-start | bytes 1572872 | tf_op jit(solution)/shard_map/ppermute | solution.py:448
  83.4 42.2 %collective-permute-start.3 = (bf16[352,2048]{1,0:T(8,128)(2,1)S(1)}, bf16[352,2048]{1,0:T(8,128)(2,1)}, u32[]{:S(2)}, u32[]{:S(2)}) collective-permute-start(bf16[352,2048]{1,0:T(8,128)(2,1)S(1)} %bitcast.32), channel_id=1, source_target_pairs={{0,64},{64,0},{128,192},{192,128},{1,65},{65,1},{129,193},{193,129... | collective-permute-start | bytes 4325384 | tf_op jit(solution)/shard_map/ppermute | solution.py:442
  83.4 42.2 %collective-permute-start.4 = (bf16[352,2048]{1,0:T(8,128)(2,1)}, bf16[352,2048]{1,0:T(8,128)(2,1)}, u32[]{:S(2)}, u32[]{:S(2)}) collective-permute-start(bf16[352,2048]{1,0:T(8,128)(2,1)} %bitcast.33), channel_id=1, source_target_pairs={{0,64},{64,0},{128,192},{192,128},{1,65},{65,1},{129,193},{193,129... | collective-permute-start | bytes 4325384 | tf_op jit(solution)/shard_map/ppermute | solution.py:442
  83.9 41.7 %collective-permute-start.5 = (bf16[352,2048]{1,0:T(8,128)(2,1)}, bf16[352,2048]{1,0:T(8,128)(2,1)}, u32[]{:S(2)}, u32[]{:S(2)}) collective-permute-start(bf16[352,2048]{1,0:T(8,128)(2,1)} %bitcast.37), channel_id=1, source_target_pairs={{0,64},{64,0},{128,192},{192,128},{1,65},{65,1},{129,193},{193,129... | collective-permute-start | bytes 4325384 | tf_op jit(solution)/shard_map/ppermute | solution.py:442
  109.0 7.6 %collective-permute-start.19 = (bf16[256,1024]{1,0:T(8,128)(2,1)S(1)}, bf16[256,1024]{1,0:T(8,128)(2,1)S(1)}, u32[]{:S(2)}, u32[]{:S(2)}) collective-permute-start(bf16[256,1024]{1,0:T(8,128)(2,1)S(1)} %collective-permute-done.18.refs_2_), channel_id=1, source_target_pairs={{0,64},{64,0},{128,192},{192,128},{1,65},{65,1},{129,193},{193,129... | collective-permute-start | bytes 1572872 | tf_op jit(solution)/shard_map/ppermute | solution.py:442
  109.0 7.6 %collective-permute-start.17 = (f32[8,256]{1,0:T(8,128)S(1)}, f32[8,256]{1,0:T(8,128)S(1)}, u32[]{:S(2)}, u32[]{:S(2)}) collective-permute-start(f32[8,256]{1,0:T(8,128)S(1)} %pad_maximum_fusion.refs_1_), channel_id=1, source_target_pairs={{0,2},{1,3},{2,0},{3,1},{4,6},{5,7},{6,4},{7,5},{8,10},{9,11},{10,... | collective-permute-start | bytes 24584 | tf_op jit(solution)/shard_map/ppermute | solution.py:448
  118.7 23.8 %all-to-all-start.4 = ((bf16[16,16,2048]{2,1,0:T(8,128)(2,1)}), bf16[16,16,2048]{2,1,0:T(8,128)(2,1)S(1)}, u32[]{:S(2)}, u32[]{:S(2)}) async-start(bf16[16,16,2048]{2,1,0:T(8,128)(2,1)} %dispatch.5), calls=%async_computation.4 | async-start | bytes 2097152 | tf_op jit(solution)/shard_map/all_to_all | solution.py:491
  143.6 32.9 %all-to-all-start.3 = ((bf16[16,32,2048]{2,1,0:T(8,128)(2,1)}), bf16[16,32,2048]{2,1,0:T(8,128)(2,1)S(1)}, u32[]{:S(2)}, u32[]{:S(2)}) async-start(bf16[16,32,2048]{2,1,0:T(8,128)(2,1)} %bitcast.45), calls=%async_computation.3 | async-start | bytes 4194304 | tf_op jit(solution)/shard_map/all_to_all | solution.py:491
  176.5 18.6 %all-to-all-start.5 = ((bf16[16,16,2048]{2,1,0:T(8,128)(2,1)}), bf16[16,16,2048]{2,1,0:T(8,128)(2,1)S(1)}, u32[]{:S(2)}, u32[]{:S(2)}) async-start(bf16[16,16,2048]{2,1,0:T(8,128)(2,1)} %bitcast.42), calls=%async_computation.5 | async-start | bytes 2097152 | tf_op jit(solution)/shard_map/all_to_all | solution.py:491
  185.2 18.3 %collective-permute-start.13 = (bf16[256,2048]{1,0:T(8,128)(2,1)}, bf16[256,2048]{1,0:T(8,128)(2,1)}, u32[]{:S(2)}, u32[]{:S(2)}) collective-permute-start(bf16[256,2048]{1,0:T(8,128)(2,1)} %get-tuple-element.36), channel_id=1, source_target_pairs={{0,64},{64,0},{128,192},{192,128},{1,65},{65,1},{129,193},{193,129... | collective-permute-start | bytes 3145736 | tf_op jit(solution)/shard_map/ppermute | solution.py:442
  195.0 24.4 %all-to-all-start.1 = ((bf16[16,16,2048]{2,1,0:T(8,128)(2,1)}), bf16[16,16,2048]{2,1,0:T(8,128)(2,1)S(1)}, u32[]{:S(2)}, u32[]{:S(2)}) async-start(bf16[16,16,2048]{2,1,0:T(8,128)(2,1)} %bitcast.41), calls=%async_computation.1 | async-start | bytes 2097152 | tf_op jit(solution)/shard_map/all_to_all | solution.py:491
  203.3 17.8 %collective-permute-start.20 = (bf16[256,1024]{1,0:T(8,128)(2,1)}, bf16[256,1024]{1,0:T(8,128)(2,1)}, u32[]{:S(2)}, u32[]{:S(2)}) collective-permute-start(bf16[256,1024]{1,0:T(8,128)(2,1)} %get-tuple-element.43), channel_id=1, source_target_pairs={{0,64},{64,0},{128,192},{192,128},{1,65},{65,1},{129,193},{193,129... | collective-permute-start | bytes 1572872 | tf_op jit(solution)/shard_map/ppermute | solution.py:442
  207.1 18.2 %collective-permute-start.14 = (bf16[256,1024]{1,0:T(8,128)(2,1)}, bf16[256,1024]{1,0:T(8,128)(2,1)}, u32[]{:S(2)}, u32[]{:S(2)}) collective-permute-start(bf16[256,1024]{1,0:T(8,128)(2,1)} %get-tuple-element.38), channel_id=1, source_target_pairs={{0,128},{64,192},{128,0},{192,64},{1,129},{65,193},{129,1},{193,65... | collective-permute-start | bytes 1572872 | tf_op jit(solution)/shard_map/ppermute | solution.py:442
  221.0 12.8 %collective-permute-start.6 = (bf16[256,1024]{1,0:T(8,128)(2,1)S(1)}, bf16[256,1024]{1,0:T(8,128)(2,1)S(1)}, u32[]{:S(2)}, u32[]{:S(2)}) collective-permute-start(bf16[256,1024]{1,0:T(8,128)(2,1)S(1)} %get-tuple-element.33), channel_id=1, source_target_pairs={{0,64},{64,0},{128,192},{192,128},{1,65},{65,1},{129,193},{193,129... | collective-permute-start | bytes 1572872 | tf_op jit(solution)/shard_map/ppermute | solution.py:442
  224.5 9.3 %collective-permute-start.21 = (bf16[256,512]{1,0:T(8,128)(2,1)S(1)}, bf16[256,512]{1,0:T(8,128)(2,1)S(1)}, u32[]{:S(2)}, u32[]{:S(2)}) collective-permute-start(bf16[256,512]{1,0:T(8,128)(2,1)S(1)} %get-tuple-element.45), channel_id=1, source_target_pairs={{0,128},{64,192},{128,0},{192,64},{1,129},{65,193},{129,1},{193,65... | collective-permute-start | bytes 786440 | tf_op jit(solution)/shard_map/ppermute | solution.py:442
  226.4 15.6 %collective-permute-start.15 = (bf16[256,1024]{1,0:T(8,128)(2,1)S(1)}, bf16[256,1024]{1,0:T(8,128)(2,1)S(1)}, u32[]{:S(2)}, u32[]{:S(2)}) collective-permute-start(bf16[256,1024]{1,0:T(8,128)(2,1)S(1)} %total.2), channel_id=1, source_target_pairs={{0,131},{64,195},{128,1},{192,65},{1,128},{65,192},{129,2},{193,66... | collective-permute-start | bytes 1572872 | tf_op jit(solution)/shard_map/ppermute | solution.py:458
  227.9 22.4 %collective-permute-start.23 = (bf16[2,256,512]{2,1,0:T(8,128)(2,1)S(1)}, bf16[2,256,512]{2,1,0:T(8,128)(2,1)S(1)}, u32[]{:S(2)}, u32[]{:S(2)}) collective-permute-start(bf16[2,256,512]{2,1,0:T(8,128)(2,1)S(1)} %get-tuple-element.47), channel_id=1, source_target_pairs={{0,64},{64,0},{128,192},{192,128},{1,65},{65,1},{129,193},{193,129... | collective-permute-start | bytes 1572872 | tf_op jit(solution)/shard_map/ppermute | solution.py:442
  228.1 22.2 %collective-permute-start.24 = (bf16[2,256,512]{2,1,0:T(8,128)(2,1)S(1)}, bf16[2,256,512]{2,1,0:T(8,128)(2,1)S(1)}, u32[]{:S(2)}, u32[]{:S(2)}) collective-permute-start(bf16[2,256,512]{2,1,0:T(8,128)(2,1)S(1)} %get-tuple-element.48), channel_id=1, source_target_pairs={{0,128},{64,192},{128,0},{192,64},{1,129},{65,193},{129,1},{193,65... | collective-permute-start | bytes 1572872 | tf_op jit(solution)/shard_map/ppermute | solution.py:442
  233.7 26.9 %collective-permute-start.25 = (bf16[2,256,512]{2,1,0:T(8,128)(2,1)S(1)}, bf16[2,256,512]{2,1,0:T(8,128)(2,1)S(1)}, u32[]{:S(2)}, u32[]{:S(2)}) collective-permute-start(bf16[2,256,512]{2,1,0:T(8,128)(2,1)S(1)} %get-tuple-element.49), channel_id=1, source_target_pairs={{0,192},{64,128},{128,64},{192,0},{1,193},{65,129},{129,65},{193,1... | collective-permute-start | bytes 1572872 | tf_op jit(solution)/shard_map/ppermute | solution.py:442
  233.8 28.8 %collective-permute-start.22 = (bf16[256,512]{1,0:T(8,128)(2,1)S(1)}, bf16[256,512]{1,0:T(8,128)(2,1)S(1)}, u32[]{:S(2)}, u32[]{:S(2)}) collective-permute-start(bf16[256,512]{1,0:T(8,128)(2,1)S(1)} %total.3), channel_id=1, source_target_pairs={{0,130},{64,194},{128,2},{192,66},{1,131},{65,195},{129,3},{193,67... | collective-permute-start | bytes 786440 | tf_op jit(solution)/shard_map/ppermute | solution.py:458
  242.7 24.2 %collective-permute-start.16 = (bf16[256,512]{1,0:T(8,128)(2,1)S(1)}, bf16[256,512]{1,0:T(8,128)(2,1)S(1)}, u32[]{:S(2)}, u32[]{:S(2)}) collective-permute-start(bf16[256,512]{1,0:T(8,128)(2,1)S(1)} %get-tuple-element.40), channel_id=1, source_target_pairs={{0,128},{64,192},{128,0},{192,64},{1,129},{65,193},{129,1},{193,65... | collective-permute-start | bytes 786440 | tf_op jit(solution)/shard_map/ppermute | solution.py:442
  (18 other events, 128.8 us)
where the time goes:
time: 270 us; the launch traced here: 268 us
  waiting for transfers between devices  130 us (48%)
  starting transfers between devices  63 us (23%)
  Pallas kernels  62.6 us (23%)
  local copies, waits for them, and re-layouts  6.67 us (2%)
  other arithmetic  4.32 us (2%)
    ppermute x6, waiting for transfers between devices, along(): return lax.ppermute(value, 'request', pairs)  51.3 us
    all_to_all x6, waiting for transfers between devices, exchange(): lax.all_to_all(value, 'request', split_axis=0, concat_axis=0, axis_index_...  36.5 us
    ppermute x18, waiting for transfers between devices, flip(): return lax.ppermute(value, 'tensor', [(i, i ^ mask) for i in range(groups)])  35.1 us
    all_to_all x6, starting transfers between devices, exchange(): lax.all_to_all(value, 'request', split_axis=0, concat_axis=0, axis_index_...  34.9 us
    pallas_call x3, Pallas kernels, expert(): pl.pallas_call(lambda *refs: expert_kernel(count // 3, *refs), in_specs=[...  30.7 us
    ppermute x18, starting transfers between devices, flip(): return lax.ppermute(value, 'tensor', [(i, i ^ mask) for i in range(groups)])  13.4 us
    ppermute x6, starting transfers between devices, along(): return lax.ppermute(value, 'request', pairs)  13.1 us
    pallas_call x1, Pallas kernels, attend(): pl.pallas_call(attend_kernel, grid_spec=pltpu.PrefetchScalarGridSpec(num_...  8.53 us
  transfers between devices with their start and end apart: 32, of which 17 were waited for; matrix products, arithmetic and copies ran while one was open for 0% of the time, Pallas kernels for 20%

commit v1 on v0

--- a/solution.py
+++ b/solution.py
@@ -25,76 +25,86 @@
     return pl.ds(pl.multiple_of(start, 128), size)
 
 
-def attend_kernel(
-    scalars_ref, q_ref, k_ref, v_ref, ck_ref, cv_ref, w_ref, keep_ref, send_ref, part_ref
-):
-    head = pl.program_id(0)
+def attend_kernel(scalars_ref, q_ref, k_ref, v_ref, ck_ref, cv_ref, w_ref, *refs):
+    outs, part_ref = refs[:-1], refs[-1]
+    group = pl.program_id(0)
     length, core = scalars_ref[0], scalars_ref[1]
-    query = q_ref[...]
     scale = HD ** (-0.5)
-    old = lax.dot_general(query, ck_ref[...], NT, preferred_element_type=jnp.float32) * scale
-    new = lax.dot_general(query, k_ref[...], NT, preferred_element_type=jnp.float32) * scale
-    old = jnp.where(lax.broadcasted_iota(jnp.int32, old.shape, 1) < length, old, neg_large)
-    rows = lax.broadcasted_iota(jnp.int32, new.shape, 0)
-    new = jnp.where(lax.broadcasted_iota(jnp.int32, new.shape, 1) <= rows, new, neg_large)
-    top = jnp.maximum(
-        jnp.max(old, axis=1, keepdims=True), jnp.max(new, axis=1, keepdims=True)
-    )
-    old = jnp.exp(old - top)
-    new = jnp.exp(new - top)
-    inverse = 1.0 / (jnp.sum(old, axis=1, keepdims=True) + jnp.sum(new, axis=1, keepdims=True))
-    attended = jnp.dot(
-        (old * inverse).astype(jnp.bfloat16), cv_ref[...], preferred_element_type=jnp.float32
-    ) + jnp.dot(
-        (new * inverse).astype(jnp.bfloat16), v_ref[...], preferred_element_type=jnp.float32
-    )
+    attended = []
+    for head in range(q_ref.shape[1] // HD):
+        own = slice(head * HD, (head + 1) * HD)
+        query = q_ref[:, own]
+        old = lax.dot_general(query, ck_ref[:, own], NT, preferred_element_type=jnp.float32) * scale
+        new = lax.dot_general(query, k_ref[:, own], NT, preferred_element_type=jnp.float32) * scale
+        old = jnp.where(lax.broadcasted_iota(jnp.int32, old.shape, 1) < length, old, neg_large)
+        rows = lax.broadcasted_iota(jnp.int32, new.shape, 0)
+        new = jnp.where(lax.broadcasted_iota(jnp.int32, new.shape, 1) <= rows, new, neg_large)
+        top = jnp.maximum(
+            jnp.max(old, axis=1, keepdims=True), jnp.max(new, axis=1, keepdims=True)
+        )
+        old = jnp.exp(old - top)
+        new = jnp.exp(new - top)
+        total = jnp.sum(old, axis=1, keepdims=True) + jnp.sum(new, axis=1, keepdims=True)
+        inverse = 1.0 / total
+        result = jnp.dot(
+            (old * inverse).astype(jnp.bfloat16), cv_ref[:, own], preferred_element_type=jnp.float32
+        ) + jnp.dot(
+            (new * inverse).astype(jnp.bfloat16), v_ref[:, own], preferred_element_type=jnp.float32
+        )
+        attended.append(result.astype(jnp.bfloat16))
     part = jnp.dot(
-        attended.astype(jnp.bfloat16), w_ref[...], preferred_element_type=jnp.float32
-    )
-
-    @pl.when(head == 0)
+        jnp.concatenate(attended, axis=1), w_ref[...], preferred_element_type=jnp.float32
+    )
+
+    @pl.when(group == 0)
     def _():
         part_ref[...] = part
 
-    @pl.when(head > 0)
+    @pl.when(group > 0)
     def _():
         part_ref[...] += part
 
-    @pl.when(head == pl.num_programs(0) - 1)
+    @pl.when(group == pl.num_programs(0) - 1)
     def _():
-        half = keep_ref.shape[1]
-        keep_ref[...] = part_ref[:, lanes(core * half, half)]
-        send_ref[...] = part_ref[:, lanes((1 - core) * half, half)].astype(jnp.bfloat16)
-
-
-def attend(scalars, span_q, span_k, span_v, cache_k, cache_v, out_proj):
+        rows, half = outs[0].shape
+        for i in range(len(outs) // 2):
+            keep_ref, send_ref = outs[2 * i : 2 * i + 2]
+            own = slice(i * rows, (i + 1) * rows)
+            keep_ref[...] = part_ref[own, lanes(core * half, half)]
+            send_ref[...] = part_ref[own, lanes((1 - core) * half, half)].astype(jnp.bfloat16)
+
+
+def attend(scalars, span_q, span_k, span_v, cache_k, cache_v, out_proj, pieces):
     span, columns = span_q.shape
     prior = cache_k.shape[0]
     width = out_proj.shape[1]
     heads = columns // HD
-    fresh = pl.BlockSpec((span, HD), lambda h, n: (0, h))
-    cached = pl.BlockSpec((prior, HD), lambda h, n: (0, h))
-    halves = pl.BlockSpec((span, width // 2), lambda h, n: (0, 0))
+    wide = 2 * HD if heads % 2 == 0 else HD
+    rows = span // pieces
+    fresh = pl.BlockSpec((span, wide), lambda h, n: (0, h))
+    cached = pl.BlockSpec((prior, wide), lambda h, n: (0, h))
+    halves = pl.BlockSpec((rows, width // 2), lambda h, n: (0, 0))
+    out = [
+        jax.ShapeDtypeStruct((rows, width // 2), jnp.float32),
+        jax.ShapeDtypeStruct((rows, width // 2), jnp.bfloat16),
+    ]
     return pl.pallas_call(
         attend_kernel,
         grid_spec=pltpu.PrefetchScalarGridSpec(
             num_scalar_prefetch=1,
-            grid=(heads,),
+            grid=(columns // wide,),
             in_specs=[
                 fresh,
                 fresh,
                 fresh,
                 cached,
                 cached,
-                pl.BlockSpec((HD, width), lambda h, n: (h, 0)),
+                pl.BlockSpec((wide, width), lambda h, n: (h, 0)),
             ],
-            out_specs=[halves, halves],
+            out_specs=[halves] * (2 * pieces),
             scratch_shapes=[pltpu.VMEM((span, width), jnp.float32)],
         ),
-        out_shape=[
-            jax.ShapeDtypeStruct((span, width // 2), jnp.float32),
-            jax.ShapeDtypeStruct((span, width // 2), jnp.bfloat16),
-        ],
+        out_shape=out * pieces,
         cost_estimate=pl.CostEstimate(
             flops=heads * span * (4 * (prior + span) * HD + 2 * HD * width),
             transcendentals=heads * span * (prior + span),
@@ -102,6 +112,28 @@
         ),
         name="attend",
     )(scalars, span_q, span_k, span_v, cache_k, cache_v, out_proj)
+
+
+def mixed_kernel(scalars_ref, hidden_ref, part_ref, came_ref, out_ref):
+    total = hidden_ref[...].astype(jnp.float32) + part_ref[...]
+    out_ref[...] = (total + came_ref[...].astype(jnp.float32)).astype(jnp.bfloat16)
+
+
+def mixed_of(scalars, piece, hidden, part, came):
+    rows, half = part.shape
+    whole = pl.BlockSpec((rows, half), lambda i, n: (0, 0))
+    return pl.pallas_call(
+        mixed_kernel,
+        grid_spec=pltpu.PrefetchScalarGridSpec(
+            num_scalar_prefetch=1,
+            grid=(1,),
+            in_specs=[pl.BlockSpec((rows, half), lambda i, n: (piece, n[1])), whole, whole],
+            out_specs=whole,
+        ),
+        out_shape=jax.ShapeDtypeStruct((rows, half), jnp.bfloat16),
+        compiler_params=pltpu.CompilerParams(vmem_limit_bytes=8 << 20),
+        name="mixed",
+    )(scalars, hidden, part, came)
 
 
 def norm_kernel(scalars_ref, mine_ref, other_ref, gain_ref, mine_out, other_out, own_out):
@@ -317,6 +349,23 @@
         compiler_params=pltpu.CompilerParams(vmem_limit_bytes=8 << 20),
         name="total",
     )(keep, came)
+
+
+def last_kernel(own_ref, keep_ref, came_ref, home_ref, out_ref):
+    total = own_ref[...].astype(jnp.float32) + keep_ref[...]
+    total = total + came_ref[...].astype(jnp.float32) + home_ref[...].astype(jnp.float32)
+    out_ref[...] = total.astype(jnp.bfloat16)
+
+
+def last(own, keep, came, home):
+    return pl.pallas_call(
+        last_kernel,
+        in_specs=[VMEM] * 4,
+        out_specs=VMEM,
+        out_shape=jax.ShapeDtypeStruct(own.shape, jnp.bfloat16),
+        compiler_params=pltpu.CompilerParams(vmem_limit_bytes=8 << 20),
+        name="last",
+    )(own, keep, came, home)
 
 
 def expert_kernel(slices, x_ref, *refs):
@@ -478,7 +527,6 @@
     groups = lax.axis_size("tensor")
     experts = lax.axis_size("request")
     plane = experts // RING
-    half = width // 2
     me = lax.axis_index("tensor")
     core = me % 2
     chip = me // 2
@@ -511,11 +559,11 @@
         cache_k[0],
         cache_v[0],
         out_proj,
+        1,
     )
     keep = keep + flip(send, 1).astype(jnp.float32)
-    keep = keep + flip(keep.astype(jnp.bfloat16), 2).astype(jnp.float32)
-    hidden_half = lax.dynamic_slice_in_dim(hidden_in, core * half, half, 1)
-    mixed_half = (hidden_half.astype(jnp.float32) + keep).astype(jnp.bfloat16)
+    came = flip(keep.astype(jnp.bfloat16), 2)
+    mixed_half = mixed_of(scalars, 0, hidden_in, keep, came)
     mine, other, own_mixed = norm(
         scalars, mixed_half, flip(mixed_half, 1), norm_gain.reshape(1, width)
     )
@@ -549,9 +597,7 @@
     keep, onward, came = gather("own", 0, chunks[0])
     keep, onward = close(scalars, keep, onward, came, homes[0])
     came = flip(onward, 2)
-    result = own_mixed.astype(jnp.float32) + keep
-    result = result + came.astype(jnp.float32) + homes[1].astype(jnp.float32)
-    layer_out = result.astype(jnp.bfloat16)
+    layer_out = last(own_mixed, keep, came, homes[1])
 
     spot = jnp.stack([me, length]).astype(jnp.int32)
     pieces = stage(spot, span_k, span_v, cache_k[0], cache_v[0], groups)

time: 270 us -> 268 us (level)
    unnamed x36 -> x38, local copies, waits for them, and re-layouts: 6.67 us -> 6.67 us
where the time goes in v1:
time: 268 us; the launch traced here: 266 us
  waiting for transfers between devices  129 us (48%)
  starting transfers between devices  63.3 us (24%)
  Pallas kernels  62.9 us (23%)
  local copies, waits for them, and re-layouts  6.67 us (2%)
    ppermute x6, waiting for transfers between devices, along(): return lax.ppermute(value, 'request', pairs)  51.1 us
    all_to_all x6, waiting for transfers between devices, exchange(): lax.all_to_all(value, 'request', split_axis=0, concat_axis=0, axis_index_...  36.5 us
    ppermute x18, waiting for transfers between devices, flip(): return lax.ppermute(value, 'tensor', [(i, i ^ mask) for i in range(groups)])  35.1 us
    all_to_all x6, starting transfers between devices, exchange(): lax.all_to_all(value, 'request', split_axis=0, concat_axis=0, axis_index_...  34.9 us
    pallas_call x3, Pallas kernels, expert(): pl.pallas_call(lambda *refs: expert_kernel(count // 3, *refs), in_specs=[...  30.7 us
    ppermute x18, starting transfers between devices, flip(): return lax.ppermute(value, 'tensor', [(i, i ^ mask) for i in range(groups)])  13.7 us
    ppermute x6, starting transfers between devices, along(): return lax.ppermute(value, 'request', pairs)  13.1 us
    pallas_call x1, Pallas kernels, attend(): pl.pallas_call(attend_kernel, grid_spec=pltpu.PrefetchScalarGridSpec(num_...  7.36 us
  transfers between devices with their start and end apart: 32, of which 17 were waited for; matrix products, arithmetic and copies ran while one was open for 0% of the time, Pallas kernels for 20%

profile of v1, /device:TPU:32, one launch (start us, length us, event | category | flops | bytes accessed | tf_op | source)
XLA Modules:
  0.0 266.0 jit_solution(3334297532279813871)
XLA Ops:
  1.9 7.4 %attend.1 = (f32[256,1024]{1,0:T(8,128)}, bf16[256,1024]{1,0:T(8,128)(2,1)}) custom-call(s32[2]{0:T(128)} %pad_add_fusion.1.scalars_ref, bf16[256,512]{1,0:T(8,128)(2,1)} %q_ref.1, bf16[256,512]{1,0:T(8,128)(2,1)} %k_ref.3, bf16[256,512]{1,0:T(8,128)(2,1)} %v_ref.3, bf16[768,512]{1,0:T(8,128)(2,1)} %bitcast.24, bf16[768,512]{1,0:T(8,128)(2,1)} %bitcast.26, ...), custom_call_target="tpu_custom_call" | custom-call | flops 1073741824 | bytes 9437184 | tf_op jit(solution)/shard_map/attend/pallas_call | solution.py:91
  14.8 12.1 %collective-permute-done.1.came_ref = bf16[256,1024]{1,0:T(8,128)(2,1)S(1)} collective-permute-done((bf16[256,1024]{1,0:T(8,128)(2,1)S(1)}, bf16[256,1024]{1,0:T(8,128)(2,1)S(1)}, u32[]{:S(2)}, u32[]{:S(2)}) %collective-permute-start.1) | collective-permute-done | bytes 524320 | tf_op jit(solution)/shard_map/ppermute | solution.py:491
  30.6 5.4 %collective-permute-start.11 = (bf16[256,1024]{1,0:T(8,128)(2,1)S(1)}, bf16[256,1024]{1,0:T(8,128)(2,1)S(1)}, u32[]{:S(2)}, u32[]{:S(2)}) collective-permute-start(bf16[256,1024]{1,0:T(8,128)(2,1)S(1)} %get-tuple-element.29.refs_2_), channel_id=1, source_target_pairs={{0,3},{1,0},{2,1},{3,2},{4,7},{5,4},{6,5},{7,6},{8,11},{9,8},{10,9... | collective-permute-start | bytes 1572872 | tf_op jit(solution)/shard_map/ppermute | solution.py:497
  38.2 7.0 %all-to-all-start = ((bf16[16,16,2048]{2,1,0:T(8,128)(2,1)}), bf16[16,16,2048]{2,1,0:T(8,128)(2,1)S(1)}, u32[]{:S(2)}, u32[]{:S(2)}) async-start(bf16[16,16,2048]{2,1,0:T(8,128)(2,1)} %dispatch.3), calls=%async_computation | async-start | bytes 2097152 | tf_op jit(solution)/shard_map/all_to_all | solution.py:539
  45.2 13.1 %collective-permute-done.11.refs_5_ = bf16[256,1024]{1,0:T(8,128)(2,1)S(1)} collective-permute-done((bf16[256,1024]{1,0:T(8,128)(2,1)S(1)}, bf16[256,1024]{1,0:T(8,128)(2,1)S(1)}, u32[]{:S(2)}, u32[]{:S(2)}) %collective-permute-start.11) | collective-permute-done | bytes 524320 | tf_op jit(solution)/shard_map/ppermute | solution.py:497
  58.3 4.6 %collective-permute-done.9.refs_2_ = bf16[256,1024]{1,0:T(8,128)(2,1)S(1)} collective-permute-done((bf16[256,1024]{1,0:T(8,128)(2,1)S(1)}, bf16[256,1024]{1,0:T(8,128)(2,1)S(1)}, u32[]{:S(2)}, u32[]{:S(2)}) %collective-permute-start.9) | collective-permute-done | bytes 524320 | tf_op jit(solution)/shard_map/ppermute | solution.py:497
  63.4 2.4 collective-permute-start.7
  69.2 2.8 %dispatch.4 = bf16[16,32,2048]{2,1,0:T(8,128)(2,1)} custom-call(s32[3]{0:T(128)S(1)} %pad_add_fusion.scalars_ref.refs_0_, f32[8,256]{1,0:T(8,128)S(1)} %collective-permute-done.7.refs_1_, bf16[256,1024]{1,0:T(8,128)(2,1)S(1)} %collective-permute-done.9.refs_2_, bf16[256,1024]{1,0:T(8,128)(2,1)S(1)} %collective-permute-done.10.refs_3_, ...), custom_call_target="tpu_custom_call" | custom-call | tf_op jit(solution)/shard_map/dispatch/pallas_call | solution.py:224
  72.0 7.3 %all-to-all-start.2 = ((bf16[16,32,2048]{2,1,0:T(8,128)(2,1)}), bf16[16,32,2048]{2,1,0:T(8,128)(2,1)}, u32[]{:S(2)}, u32[]{:S(2)}) async-start(bf16[16,32,2048]{2,1,0:T(8,128)(2,1)} %dispatch.4), calls=%async_computation.2 | async-start | bytes 4194304 | tf_op jit(solution)/shard_map/all_to_all | solution.py:539
  79.3 2.4 collective-permute-start.18
  82.5 24.8 %collective-permute-done.18.refs_2_ = bf16[256,1024]{1,0:T(8,128)(2,1)S(1)} collective-permute-done((bf16[256,1024]{1,0:T(8,128)(2,1)S(1)}, bf16[256,1024]{1,0:T(8,128)(2,1)S(1)}, u32[]{:S(2)}, u32[]{:S(2)}) %collective-permute-start.18) | collective-permute-done | bytes 524320 | tf_op jit(solution)/shard_map/ppermute | solution.py:497
  107.3 2.4 collective-permute-start.17
  109.7 5.2 %collective-permute-done.17.refs_1_ = f32[8,256]{1,0:T(8,128)S(1)} collective-permute-done((f32[8,256]{1,0:T(8,128)S(1)}, f32[8,256]{1,0:T(8,128)S(1)}, u32[]{:S(2)}, u32[]{:S(2)}) %collective-permute-start.17) | collective-permute-done | bytes 8224 | tf_op jit(solution)/shard_map/ppermute | solution.py:497
  114.9 2.2 dispatch.5
  117.1 6.8 %all-to-all-start.4 = ((bf16[16,16,2048]{2,1,0:T(8,128)(2,1)}), bf16[16,16,2048]{2,1,0:T(8,128)(2,1)S(1)}, u32[]{:S(2)}, u32[]{:S(2)}) async-start(bf16[16,16,2048]{2,1,0:T(8,128)(2,1)} %dispatch.5), calls=%async_computation.4 | async-start | bytes 2097152 | tf_op jit(solution)/shard_map/all_to_all | solution.py:539
  123.9 13.9 %expert.4 = bf16[512,2048]{1,0:T(8,128)(2,1)} custom-call(bf16[512,2048]{1,0:T(8,128)(2,1)} %bitcast.17.refs_0_, bf16[352,2048]{1,0:T(8,128)(2,1)} %bitcast.29, bf16[352,2048]{1,0:T(8,128)(2,1)} %bitcast.34, bf16[352,2048]{1,0:T(8,128)(2,1)} %bitcast.38, bf16[352,2048]{1,0:T(8,128)(2,1)} %collective-permute-done.3.refs_4_, ...), custom_call_target="tpu_custom_call" | custom-call | flops 4429185024 | bytes 12845056 | tf_op jit(solution)/shard_map/expert/pallas_call | solution.py:421
  137.8 3.1 %all-to-all-done.4 = bf16[16,16,2048]{2,1,0:T(8,128)(2,1)S(1)} async-done(((bf16[16,16,2048]{2,1,0:T(8,128)(2,1)}), bf16[16,16,2048]{2,1,0:T(8,128)(2,1)S(1)}, u32[]{:S(2)}, u32[]{:S(2)}) %all-to-all-start.4) | async-done | bytes 1048608 | tf_op jit(solution)/shard_map/all_to_all | solution.py:539
  142.0 4.1 %all-to-all-start.3 = ((bf16[16,32,2048]{2,1,0:T(8,128)(2,1)}), bf16[16,32,2048]{2,1,0:T(8,128)(2,1)S(1)}, u32[]{:S(2)}, u32[]{:S(2)}) async-start(bf16[16,32,2048]{2,1,0:T(8,128)(2,1)} %bitcast.46), calls=%async_computation.3 | async-start | bytes 4194304 | tf_op jit(solution)/shard_map/all_to_all | solution.py:539
  146.1 8.4 %expert.5 = bf16[256,2048]{1,0:T(8,128)(2,1)} custom-call(bf16[256,2048]{1,0:T(8,128)(2,1)} %bitcast.44, bf16[352,2048]{1,0:T(8,128)(2,1)} %bitcast.30, bf16[352,2048]{1,0:T(8,128)(2,1)} %bitcast.35, bf16[352,2048]{1,0:T(8,128)(2,1)} %bitcast.39, bf16[352,2048]{1,0:T(8,128)(2,1)} %collective-permute-done.3.refs_4_, ...), custom_call_target="tpu_custom_call" | custom-call | flops 2214592512 | bytes 10747904 | tf_op jit(solution)/shard_map/expert/pallas_call | solution.py:421
  154.5 20.3 %all-to-all-done.3.refs_3_ = bf16[16,32,2048]{2,1,0:T(8,128)(2,1)S(1)} async-done(((bf16[16,32,2048]{2,1,0:T(8,128)(2,1)}), bf16[16,32,2048]{2,1,0:T(8,128)(2,1)S(1)}, u32[]{:S(2)}, u32[]{:S(2)}) %all-to-all-start.3) | async-done | bytes 2097184 | tf_op jit(solution)/shard_map/all_to_all | solution.py:539
  174.8 3.7 %all-to-all-start.5 = ((bf16[16,16,2048]{2,1,0:T(8,128)(2,1)}), bf16[16,16,2048]{2,1,0:T(8,128)(2,1)S(1)}, u32[]{:S(2)}, u32[]{:S(2)}) async-start(bf16[16,16,2048]{2,1,0:T(8,128)(2,1)} %bitcast.43), calls=%async_computation.5 | async-start | bytes 2097152 | tf_op jit(solution)/shard_map/all_to_all | solution.py:539
  178.5 3.0 %combine.4 = (f32[256,1024]{1,0:T(8,128)S(1)}, f32[256,1024]{1,0:T(8,128)S(1)}, bf16[256,2048]{1,0:T(8,128)(2,1)}) custom-call(s32[3]{0:T(128)S(1)} %pad_add_fusion.scalars_ref.refs_0_, f32[8,256]{1,0:T(8,128)S(1)} %collective-permute-done.7.refs_1_, f32[8,256]{1,0:T(8,128)S(1)} %collective-permute-done.8.refs_4_.refs_2_, ...), custom_call_target="tpu_custom_call" | custom-call | tf_op jit(solution)/shard_map/combine/pallas_call | solution.py:280
  183.6 8.4 %expert.3 = bf16[256,2048]{1,0:T(8,128)(2,1)} custom-call(bf16[256,2048]{1,0:T(8,128)(2,1)} %bitcast.41, bf16[352,2048]{1,0:T(8,128)(2,1)} %bitcast.31, bf16[352,2048]{1,0:T(8,128)(2,1)} %bitcast.36, bf16[352,2048]{1,0:T(8,128)(2,1)} %bitcast.40, bf16[352,2048]{1,0:T(8,128)(2,1)} %collective-permute-done.3.refs_4_, ...), custom_call_target="tpu_custom_call" | custom-call | flops 2214592512 | bytes 10747904 | tf_op jit(solution)/shard_map/expert/pallas_call | solution.py:421
  193.4 6.0 %all-to-all-start.1 = ((bf16[16,16,2048]{2,1,0:T(8,128)(2,1)}), bf16[16,16,2048]{2,1,0:T(8,128)(2,1)S(1)}, u32[]{:S(2)}, u32[]{:S(2)}) async-start(bf16[16,16,2048]{2,1,0:T(8,128)(2,1)} %bitcast.42), calls=%async_computation.1 | async-start | bytes 2097152 | tf_op jit(solution)/shard_map/all_to_all | solution.py:539
  199.4 2.3 combine.5
  203.2 2.2 fold.2
  206.1 11.7 %all-to-all-done.1.refs_2_ = bf16[16,16,2048]{2,1,0:T(8,128)(2,1)S(1)} async-done(((bf16[16,16,2048]{2,1,0:T(8,128)(2,1)}), bf16[16,16,2048]{2,1,0:T(8,128)(2,1)S(1)}, u32[]{:S(2)}, u32[]{:S(2)}) %all-to-all-start.1) | async-done | bytes 1048608 | tf_op jit(solution)/shard_map/all_to_all | solution.py:539
  227.7 4.3 %collective-permute-done.21.came_ref = bf16[256,512]{1,0:T(8,128)(2,1)S(1)} collective-permute-done((bf16[256,512]{1,0:T(8,128)(2,1)S(1)}, bf16[256,512]{1,0:T(8,128)(2,1)S(1)}, u32[]{:S(2)}, u32[]{:S(2)}) %collective-permute-start.21) | collective-permute-done | bytes 262176 | tf_op jit(solution)/shard_map/ppermute | solution.py:491
  233.7 6.6 %collective-permute-done.15.home_ref = bf16[256,1024]{1,0:T(8,128)(2,1)S(1)} collective-permute-done((bf16[256,1024]{1,0:T(8,128)(2,1)S(1)}, bf16[256,1024]{1,0:T(8,128)(2,1)S(1)}, u32[]{:S(2)}, u32[]{:S(2)}) %collective-permute-start.15) | collective-permute-done | bytes 524320 | tf_op jit(solution)/shard_map/ppermute | solution.py:507
  241.0 7.6 %collective-permute-start.16 = (bf16[256,512]{1,0:T(8,128)(2,1)S(1)}, bf16[256,512]{1,0:T(8,128)(2,1)S(1)}, u32[]{:S(2)}, u32[]{:S(2)}) collective-permute-start(bf16[256,512]{1,0:T(8,128)(2,1)S(1)} %get-tuple-element.40), channel_id=1, source_target_pairs={{0,128},{64,192},{128,0},{192,64},{1,129},{65,193},{129,1},{193,65... | collective-permute-start | bytes 786440 | tf_op jit(solution)/shard_map/ppermute | solution.py:491
  248.6 10.4 %collective-permute-done.25.refs_3_ = bf16[2,256,512]{2,1,0:T(8,128)(2,1)S(1)} collective-permute-done((bf16[2,256,512]{2,1,0:T(8,128)(2,1)S(1)}, bf16[2,256,512]{2,1,0:T(8,128)(2,1)S(1)}, u32[]{:S(2)}, u32[]{:S(2)}) %collective-permute-start.25) | collective-permute-done | bytes 524320 | tf_op jit(solution)/shard_map/ppermute | solution.py:491
  261.0 4.2 %collective-permute-done.16.came_ref = bf16[256,512]{1,0:T(8,128)(2,1)S(1)} collective-permute-done((bf16[256,512]{1,0:T(8,128)(2,1)S(1)}, bf16[256,512]{1,0:T(8,128)(2,1)S(1)}, u32[]{:S(2)}, u32[]{:S(2)}) %collective-permute-start.16) | collective-permute-done | bytes 262176 | tf_op jit(solution)/shard_map/ppermute | solution.py:491
  (96 shorter events, 38.3 us)
Async XLA Ops:
  9.2 2.1 collective-permute-start
  12.8 14.1 %collective-permute-start.1 = (bf16[256,1024]{1,0:T(8,128)(2,1)S(1)}, bf16[256,1024]{1,0:T(8,128)(2,1)S(1)}, u32[]{:S(2)}, u32[]{:S(2)}) collective-permute-start(bf16[256,1024]{1,0:T(8,128)(2,1)S(1)} %get-tuple-element.50), channel_id=1, source_target_pairs={{0,128},{64,192},{128,0},{192,64},{1,129},{65,193},{129,1},{193,65... | collective-permute-start | bytes 1572872 | tf_op jit(solution)/shard_map/ppermute | solution.py:491
  27.6 2.0 collective-permute-start.2
  30.6 27.7 %collective-permute-start.11 = (bf16[256,1024]{1,0:T(8,128)(2,1)S(1)}, bf16[256,1024]{1,0:T(8,128)(2,1)S(1)}, u32[]{:S(2)}, u32[]{:S(2)}) collective-permute-start(bf16[256,1024]{1,0:T(8,128)(2,1)S(1)} %get-tuple-element.29.refs_2_), channel_id=1, source_target_pairs={{0,3},{1,0},{2,1},{3,2},{4,7},{5,4},{6,5},{7,6},{8,11},{9,8},{10,9... | collective-permute-start | bytes 1572872 | tf_op jit(solution)/shard_map/ppermute | solution.py:497
  36.0 26.9 %collective-permute-start.9 = (bf16[256,1024]{1,0:T(8,128)(2,1)S(1)}, bf16[256,1024]{1,0:T(8,128)(2,1)S(1)}, u32[]{:S(2)}, u32[]{:S(2)}) collective-permute-start(bf16[256,1024]{1,0:T(8,128)(2,1)S(1)} %get-tuple-element.29.refs_2_), channel_id=1, source_target_pairs={{0,1},{1,2},{2,3},{3,0},{4,5},{5,6},{6,7},{7,4},{8,9},{9,10},{10,1... | collective-permute-start | bytes 1572872 | tf_op jit(solution)/shard_map/ppermute | solution.py:497
  38.2 33.9 %all-to-all-start = ((bf16[16,16,2048]{2,1,0:T(8,128)(2,1)}), bf16[16,16,2048]{2,1,0:T(8,128)(2,1)S(1)}, u32[]{:S(2)}, u32[]{:S(2)}) async-start(bf16[16,16,2048]{2,1,0:T(8,128)(2,1)} %dispatch.3), calls=%async_computation | async-start | bytes 2097152 | tf_op jit(solution)/shard_map/all_to_all | solution.py:539
  58.3 10.9 %collective-permute-start.12 = (bf16[256,1024]{1,0:T(8,128)(2,1)S(1)}, bf16[256,1024]{1,0:T(8,128)(2,1)S(1)}, u32[]{:S(2)}, u32[]{:S(2)}) collective-permute-start(bf16[256,1024]{1,0:T(8,128)(2,1)S(1)} %collective-permute-done.11.refs_5_), channel_id=1, source_target_pairs={{0,64},{64,0},{128,192},{192,128},{1,65},{65,1},{129,193},{193,129... | collective-permute-start | bytes 1572872 | tf_op jit(solution)/shard_map/ppermute | solution.py:491
  62.9 6.3 %collective-permute-start.10 = (bf16[256,1024]{1,0:T(8,128)(2,1)S(1)}, bf16[256,1024]{1,0:T(8,128)(2,1)S(1)}, u32[]{:S(2)}, u32[]{:S(2)}) collective-permute-start(bf16[256,1024]{1,0:T(8,128)(2,1)S(1)} %collective-permute-done.9.refs_2_), channel_id=1, source_target_pairs={{0,64},{64,0},{128,192},{192,128},{1,65},{65,1},{129,193},{193,129... | collective-permute-start | bytes 1572872 | tf_op jit(solution)/shard_map/ppermute | solution.py:491
  62.9 4.6 %collective-permute-start.8 = (f32[8,256]{1,0:T(8,128)S(1)}, f32[8,256]{1,0:T(8,128)S(1)}, u32[]{:S(2)}, u32[]{:S(2)}) collective-permute-start(f32[8,256]{1,0:T(8,128)S(1)} %pad_maximum_fusion.refs_1_), channel_id=1, source_target_pairs={{0,3},{1,0},{2,1},{3,2},{4,7},{5,4},{6,5},{7,6},{8,11},{9,8},{10,9... | collective-permute-start | bytes 24584 | tf_op jit(solution)/shard_map/ppermute | solution.py:497
  63.4 5.8 %collective-permute-start.7 = (f32[8,256]{1,0:T(8,128)S(1)}, f32[8,256]{1,0:T(8,128)S(1)}, u32[]{:S(2)}, u32[]{:S(2)}) collective-permute-start(f32[8,256]{1,0:T(8,128)S(1)} %pad_maximum_fusion.refs_1_), channel_id=1, source_target_pairs={{0,1},{1,2},{2,3},{3,0},{4,5},{5,6},{6,7},{7,4},{8,9},{9,10},{10,1... | collective-permute-start | bytes 24584 | tf_op jit(solution)/shard_map/ppermute | solution.py:497
  72.0 45.0 %all-to-all-start.2 = ((bf16[16,32,2048]{2,1,0:T(8,128)(2,1)}), bf16[16,32,2048]{2,1,0:T(8,128)(2,1)}, u32[]{:S(2)}, u32[]{:S(2)}) async-start(bf16[16,32,2048]{2,1,0:T(8,128)(2,1)} %dispatch.4), calls=%async_computation.2 | async-start | bytes 4194304 | tf_op jit(solution)/shard_map/all_to_all | solution.py:539
  79.3 28.0 %collective-permute-start.18 = (bf16[256,1024]{1,0:T(8,128)(2,1)S(1)}, bf16[256,1024]{1,0:T(8,128)(2,1)S(1)}, u32[]{:S(2)}, u32[]{:S(2)}) collective-permute-start(bf16[256,1024]{1,0:T(8,128)(2,1)S(1)} %get-tuple-element.29.refs_2_), channel_id=1, source_target_pairs={{0,2},{1,3},{2,0},{3,1},{4,6},{5,7},{6,4},{7,5},{8,10},{9,11},{10,... | collective-permute-start | bytes 1572872 | tf_op jit(solution)/shard_map/ppermute | solution.py:497
  81.7 42.2 %collective-permute-start.3 = (bf16[352,2048]{1,0:T(8,128)(2,1)S(1)}, bf16[352,2048]{1,0:T(8,128)(2,1)}, u32[]{:S(2)}, u32[]{:S(2)}) collective-permute-start(bf16[352,2048]{1,0:T(8,128)(2,1)S(1)} %bitcast.32), channel_id=1, source_target_pairs={{0,64},{64,0},{128,192},{192,128},{1,65},{65,1},{129,193},{193,129... | collective-permute-start | bytes 4325384 | tf_op jit(solution)/shard_map/ppermute | solution.py:491
  81.7 42.2 %collective-permute-start.4 = (bf16[352,2048]{1,0:T(8,128)(2,1)}, bf16[352,2048]{1,0:T(8,128)(2,1)}, u32[]{:S(2)}, u32[]{:S(2)}) collective-permute-start(bf16[352,2048]{1,0:T(8,128)(2,1)} %bitcast.33), channel_id=1, source_target_pairs={{0,64},{64,0},{128,192},{192,128},{1,65},{65,1},{129,193},{193,129... | collective-permute-start | bytes 4325384 | tf_op jit(solution)/shard_map/ppermute | solution.py:491
  82.2 41.7 %collective-permute-start.5 = (bf16[352,2048]{1,0:T(8,128)(2,1)}, bf16[352,2048]{1,0:T(8,128)(2,1)}, u32[]{:S(2)}, u32[]{:S(2)}) collective-permute-start(bf16[352,2048]{1,0:T(8,128)(2,1)} %bitcast.37), channel_id=1, source_target_pairs={{0,64},{64,0},{128,192},{192,128},{1,65},{65,1},{129,193},{193,129... | collective-permute-start | bytes 4325384 | tf_op jit(solution)/shard_map/ppermute | solution.py:491
  107.3 7.6 %collective-permute-start.19 = (bf16[256,1024]{1,0:T(8,128)(2,1)S(1)}, bf16[256,1024]{1,0:T(8,128)(2,1)S(1)}, u32[]{:S(2)}, u32[]{:S(2)}) collective-permute-start(bf16[256,1024]{1,0:T(8,128)(2,1)S(1)} %collective-permute-done.18.refs_2_), channel_id=1, source_target_pairs={{0,64},{64,0},{128,192},{192,128},{1,65},{65,1},{129,193},{193,129... | collective-permute-start | bytes 1572872 | tf_op jit(solution)/shard_map/ppermute | solution.py:491
  107.3 7.6 %collective-permute-start.17 = (f32[8,256]{1,0:T(8,128)S(1)}, f32[8,256]{1,0:T(8,128)S(1)}, u32[]{:S(2)}, u32[]{:S(2)}) collective-permute-start(f32[8,256]{1,0:T(8,128)S(1)} %pad_maximum_fusion.refs_1_), channel_id=1, source_target_pairs={{0,2},{1,3},{2,0},{3,1},{4,6},{5,7},{6,4},{7,5},{8,10},{9,11},{10,... | collective-permute-start | bytes 24584 | tf_op jit(solution)/shard_map/ppermute | solution.py:497
  117.1 23.8 %all-to-all-start.4 = ((bf16[16,16,2048]{2,1,0:T(8,128)(2,1)}), bf16[16,16,2048]{2,1,0:T(8,128)(2,1)S(1)}, u32[]{:S(2)}, u32[]{:S(2)}) async-start(bf16[16,16,2048]{2,1,0:T(8,128)(2,1)} %dispatch.5), calls=%async_computation.4 | async-start | bytes 2097152 | tf_op jit(solution)/shard_map/all_to_all | solution.py:539
  142.0 32.9 %all-to-all-start.3 = ((bf16[16,32,2048]{2,1,0:T(8,128)(2,1)}), bf16[16,32,2048]{2,1,0:T(8,128)(2,1)S(1)}, u32[]{:S(2)}, u32[]{:S(2)}) async-start(bf16[16,32,2048]{2,1,0:T(8,128)(2,1)} %bitcast.46), calls=%async_computation.3 | async-start | bytes 4194304 | tf_op jit(solution)/shard_map/all_to_all | solution.py:539
  174.8 18.6 %all-to-all-start.5 = ((bf16[16,16,2048]{2,1,0:T(8,128)(2,1)}), bf16[16,16,2048]{2,1,0:T(8,128)(2,1)S(1)}, u32[]{:S(2)}, u32[]{:S(2)}) async-start(bf16[16,16,2048]{2,1,0:T(8,128)(2,1)} %bitcast.43), calls=%async_computation.5 | async-start | bytes 2097152 | tf_op jit(solution)/shard_map/all_to_all | solution.py:539
  183.6 18.3 %collective-permute-start.13 = (bf16[256,2048]{1,0:T(8,128)(2,1)}, bf16[256,2048]{1,0:T(8,128)(2,1)}, u32[]{:S(2)}, u32[]{:S(2)}) collective-permute-start(bf16[256,2048]{1,0:T(8,128)(2,1)} %get-tuple-element.36), channel_id=1, source_target_pairs={{0,64},{64,0},{128,192},{192,128},{1,65},{65,1},{129,193},{193,129... | collective-permute-start | bytes 3145736 | tf_op jit(solution)/shard_map/ppermute | solution.py:491
  193.4 24.4 %all-to-all-start.1 = ((bf16[16,16,2048]{2,1,0:T(8,128)(2,1)}), bf16[16,16,2048]{2,1,0:T(8,128)(2,1)S(1)}, u32[]{:S(2)}, u32[]{:S(2)}) async-start(bf16[16,16,2048]{2,1,0:T(8,128)(2,1)} %bitcast.42), calls=%async_computation.1 | async-start | bytes 2097152 | tf_op jit(solution)/shard_map/all_to_all | solution.py:539
  201.6 17.8 %collective-permute-start.20 = (bf16[256,1024]{1,0:T(8,128)(2,1)}, bf16[256,1024]{1,0:T(8,128)(2,1)}, u32[]{:S(2)}, u32[]{:S(2)}) collective-permute-start(bf16[256,1024]{1,0:T(8,128)(2,1)} %get-tuple-element.43), channel_id=1, source_target_pairs={{0,64},{64,0},{128,192},{192,128},{1,65},{65,1},{129,193},{193,129... | collective-permute-start | bytes 1572872 | tf_op jit(solution)/shard_map/ppermute | solution.py:491
  205.4 18.2 %collective-permute-start.14 = (bf16[256,1024]{1,0:T(8,128)(2,1)}, bf16[256,1024]{1,0:T(8,128)(2,1)}, u32[]{:S(2)}, u32[]{:S(2)}) collective-permute-start(bf16[256,1024]{1,0:T(8,128)(2,1)} %get-tuple-element.38), channel_id=1, source_target_pairs={{0,128},{64,192},{128,0},{192,64},{1,129},{65,193},{129,1},{193,65... | collective-permute-start | bytes 1572872 | tf_op jit(solution)/shard_map/ppermute | solution.py:491
  219.4 12.8 %collective-permute-start.6 = (bf16[256,1024]{1,0:T(8,128)(2,1)S(1)}, bf16[256,1024]{1,0:T(8,128)(2,1)S(1)}, u32[]{:S(2)}, u32[]{:S(2)}) collective-permute-start(bf16[256,1024]{1,0:T(8,128)(2,1)S(1)} %get-tuple-element.33), channel_id=1, source_target_pairs={{0,64},{64,0},{128,192},{192,128},{1,65},{65,1},{129,193},{193,129... | collective-permute-start | bytes 1572872 | tf_op jit(solution)/shard_map/ppermute | solution.py:491
  222.8 9.3 %collective-permute-start.21 = (bf16[256,512]{1,0:T(8,128)(2,1)S(1)}, bf16[256,512]{1,0:T(8,128)(2,1)S(1)}, u32[]{:S(2)}, u32[]{:S(2)}) collective-permute-start(bf16[256,512]{1,0:T(8,128)(2,1)S(1)} %get-tuple-element.45), channel_id=1, source_target_pairs={{0,128},{64,192},{128,0},{192,64},{1,129},{65,193},{129,1},{193,65... | collective-permute-start | bytes 786440 | tf_op jit(solution)/shard_map/ppermute | solution.py:491
  224.8 15.6 %collective-permute-start.15 = (bf16[256,1024]{1,0:T(8,128)(2,1)S(1)}, bf16[256,1024]{1,0:T(8,128)(2,1)S(1)}, u32[]{:S(2)}, u32[]{:S(2)}) collective-permute-start(bf16[256,1024]{1,0:T(8,128)(2,1)S(1)} %total.2), channel_id=1, source_target_pairs={{0,131},{64,195},{128,1},{192,65},{1,128},{65,192},{129,2},{193,66... | collective-permute-start | bytes 1572872 | tf_op jit(solution)/shard_map/ppermute | solution.py:507
  226.2 22.4 %collective-permute-start.23 = (bf16[2,256,512]{2,1,0:T(8,128)(2,1)S(1)}, bf16[2,256,512]{2,1,0:T(8,128)(2,1)S(1)}, u32[]{:S(2)}, u32[]{:S(2)}) collective-permute-start(bf16[2,256,512]{2,1,0:T(8,128)(2,1)S(1)} %get-tuple-element.47), channel_id=1, source_target_pairs={{0,64},{64,0},{128,192},{192,128},{1,65},{65,1},{129,193},{193,129... | collective-permute-start | bytes 1572872 | tf_op jit(solution)/shard_map/ppermute | solution.py:491
  226.4 22.2 %collective-permute-start.24 = (bf16[2,256,512]{2,1,0:T(8,128)(2,1)S(1)}, bf16[2,256,512]{2,1,0:T(8,128)(2,1)S(1)}, u32[]{:S(2)}, u32[]{:S(2)}) collective-permute-start(bf16[2,256,512]{2,1,0:T(8,128)(2,1)S(1)} %get-tuple-element.48), channel_id=1, source_target_pairs={{0,128},{64,192},{128,0},{192,64},{1,129},{65,193},{129,1},{193,65... | collective-permute-start | bytes 1572872 | tf_op jit(solution)/shard_map/ppermute | solution.py:491
  232.1 26.9 %collective-permute-start.25 = (bf16[2,256,512]{2,1,0:T(8,128)(2,1)S(1)}, bf16[2,256,512]{2,1,0:T(8,128)(2,1)S(1)}, u32[]{:S(2)}, u32[]{:S(2)}) collective-permute-start(bf16[2,256,512]{2,1,0:T(8,128)(2,1)S(1)} %get-tuple-element.49), channel_id=1, source_target_pairs={{0,192},{64,128},{128,64},{192,0},{1,193},{65,129},{129,65},{193,1... | collective-permute-start | bytes 1572872 | tf_op jit(solution)/shard_map/ppermute | solution.py:491
  232.2 28.8 %collective-permute-start.22 = (bf16[256,512]{1,0:T(8,128)(2,1)S(1)}, bf16[256,512]{1,0:T(8,128)(2,1)S(1)}, u32[]{:S(2)}, u32[]{:S(2)}) collective-permute-start(bf16[256,512]{1,0:T(8,128)(2,1)S(1)} %total.3), channel_id=1, source_target_pairs={{0,130},{64,194},{128,2},{192,66},{1,131},{65,195},{129,3},{193,67... | collective-permute-start | bytes 786440 | tf_op jit(solution)/shard_map/ppermute | solution.py:507
  241.0 24.2 %collective-permute-start.16 = (bf16[256,512]{1,0:T(8,128)(2,1)S(1)}, bf16[256,512]{1,0:T(8,128)(2,1)S(1)}, u32[]{:S(2)}, u32[]{:S(2)}) collective-permute-start(bf16[256,512]{1,0:T(8,128)(2,1)S(1)} %get-tuple-element.40), channel_id=1, source_target_pairs={{0,128},{64,192},{128,0},{192,64},{1,129},{65,193},{129,1},{193,65... | collective-permute-start | bytes 786440 | tf_op jit(solution)/shard_map/ppermute | solution.py:491
  (19 other events, 124.4 us)

commit v2 on v1

--- a/solution.py
+++ b/solution.py
@@ -336,6 +336,26 @@
     )(keep, onward, came)
 
 
+def sum_kernel(keep_ref, came_ref, keep_out, send_out):
+    total = keep_ref[...] + came_ref[...].astype(jnp.float32)
+    keep_out[...] = total
+    send_out[...] = total.astype(jnp.bfloat16)
+
+
+def sum_of(keep, came):
+    return pl.pallas_call(
+        sum_kernel,
+        in_specs=[VMEM] * 2,
+        out_specs=[VMEM] * 2,
+        out_shape=[
+            jax.ShapeDtypeStruct(keep.shape, jnp.float32),
+            jax.ShapeDtypeStruct(keep.shape, jnp.bfloat16),
+        ],
+        compiler_params=pltpu.CompilerParams(vmem_limit_bytes=8 << 20),
+        name="sum",
+    )(keep, came)
+
+
 def total_kernel(keep_ref, came_ref, out_ref):
     out_ref[...] = (keep_ref[...] + came_ref[...].astype(jnp.float32)).astype(jnp.bfloat16)
 
@@ -561,8 +581,8 @@
         out_proj,
         1,
     )
-    keep = keep + flip(send, 1).astype(jnp.float32)
-    came = flip(keep.astype(jnp.bfloat16), 2)
+    keep, send = sum_of(keep, flip(send, 1))
+    came = flip(send, 2)
     mixed_half = mixed_of(scalars, 0, hidden_in, keep, came)
     mine, other, own_mixed = norm(
         scalars, mixed_half, flip(mixed_half, 1), norm_gain.reshape(1, width)

time: 268 us -> 268 us (level)
    unnamed x38 -> x40, local copies, waits for them, and re-layouts: 6.67 us -> 7.88 us
where the time goes in v2:
time: 268 us; the launch traced here: 266 us
  waiting for transfers between devices  129 us (48%)
  starting transfers between devices  63.3 us (24%)
  Pallas kernels  63.2 us (24%)
  local copies, waits for them, and re-layouts  7.88 us (3%)
    ppermute x6, waiting for transfers between devices, along(): return lax.ppermute(value, 'request', pairs)  51.1 us
    all_to_all x6, waiting for transfers between devices, exchange(): lax.all_to_all(value, 'request', split_axis=0, concat_axis=0, axis_index_...  36.5 us
    ppermute x18, waiting for transfers between devices, flip(): return lax.ppermute(value, 'tensor', [(i, i ^ mask) for i in range(groups)])  35.1 us
    all_to_all x6, starting transfers between devices, exchange(): lax.all_to_all(value, 'request', split_axis=0, concat_axis=0, axis_index_...  35 us
    pallas_call x3, Pallas kernels, expert(): pl.pallas_call(lambda *refs: expert_kernel(count // 3, *refs), in_specs=[...  30.7 us
    ppermute x18, starting transfers between devices, flip(): return lax.ppermute(value, 'tensor', [(i, i ^ mask) for i in range(groups)])  13.7 us
    ppermute x6, starting transfers between devices, along(): return lax.ppermute(value, 'request', pairs)  13.1 us
    unnamed x40, local copies, waits for them, and re-layouts  7.88 us
  transfers between devices with their start and end apart: 32, of which 17 were waited for; matrix products, arithmetic and copies ran while one was open for 0% of the time, Pallas kernels for 20%

profile of v2, /device:TPU:32, one launch (start us, length us, event | category | flops | bytes accessed | tf_op | source)
XLA Modules:
  0.0 266.1 jit_solution(1291347150060428372)
XLA Ops:
  1.9 7.5 %attend.1 = (f32[256,1024]{1,0:T(8,128)}, bf16[256,1024]{1,0:T(8,128)(2,1)}) custom-call(s32[2]{0:T(128)} %pad_add_fusion.1.scalars_ref, bf16[256,512]{1,0:T(8,128)(2,1)} %q_ref.1, bf16[256,512]{1,0:T(8,128)(2,1)} %k_ref.3, bf16[256,512]{1,0:T(8,128)(2,1)} %v_ref.3, bf16[768,512]{1,0:T(8,128)(2,1)} %bitcast.24, bf16[768,512]{1,0:T(8,128)(2,1)} %bitcast.26, ...), custom_call_target="tpu_custom_call" | custom-call | flops 1073741824 | bytes 9437184 | tf_op jit(solution)/shard_map/attend/pallas_call | solution.py:91
  14.8 12.1 %collective-permute-done.1.came_ref = bf16[256,1024]{1,0:T(8,128)(2,1)S(1)} collective-permute-done((bf16[256,1024]{1,0:T(8,128)(2,1)S(1)}, bf16[256,1024]{1,0:T(8,128)(2,1)S(1)}, u32[]{:S(2)}, u32[]{:S(2)}) %collective-permute-start.1) | collective-permute-done | bytes 524320 | tf_op jit(solution)/shard_map/ppermute | solution.py:511
  30.7 5.4 %collective-permute-start.11 = (bf16[256,1024]{1,0:T(8,128)(2,1)S(1)}, bf16[256,1024]{1,0:T(8,128)(2,1)S(1)}, u32[]{:S(2)}, u32[]{:S(2)}) collective-permute-start(bf16[256,1024]{1,0:T(8,128)(2,1)S(1)} %get-tuple-element.33.refs_2_), channel_id=1, source_target_pairs={{0,3},{1,0},{2,1},{3,2},{4,7},{5,4},{6,5},{7,6},{8,11},{9,8},{10,9... | collective-permute-start | bytes 1572872 | tf_op jit(solution)/shard_map/ppermute | solution.py:517
  38.2 7.0 %all-to-all-start = ((bf16[16,16,2048]{2,1,0:T(8,128)(2,1)}), bf16[16,16,2048]{2,1,0:T(8,128)(2,1)S(1)}, u32[]{:S(2)}, u32[]{:S(2)}) async-start(bf16[16,16,2048]{2,1,0:T(8,128)(2,1)} %dispatch.3), calls=%async_computation | async-start | bytes 2097152 | tf_op jit(solution)/shard_map/all_to_all | solution.py:559
  45.3 13.1 %collective-permute-done.11.refs_5_ = bf16[256,1024]{1,0:T(8,128)(2,1)S(1)} collective-permute-done((bf16[256,1024]{1,0:T(8,128)(2,1)S(1)}, bf16[256,1024]{1,0:T(8,128)(2,1)S(1)}, u32[]{:S(2)}, u32[]{:S(2)}) %collective-permute-start.11) | collective-permute-done | bytes 524320 | tf_op jit(solution)/shard_map/ppermute | solution.py:517
  58.4 4.7 %collective-permute-done.9.refs_2_ = bf16[256,1024]{1,0:T(8,128)(2,1)S(1)} collective-permute-done((bf16[256,1024]{1,0:T(8,128)(2,1)S(1)}, bf16[256,1024]{1,0:T(8,128)(2,1)S(1)}, u32[]{:S(2)}, u32[]{:S(2)}) %collective-permute-start.9) | collective-permute-done | bytes 524320 | tf_op jit(solution)/shard_map/ppermute | solution.py:517
  63.5 2.5 collective-permute-start.7
  69.3 2.8 %dispatch.4 = bf16[16,32,2048]{2,1,0:T(8,128)(2,1)} custom-call(s32[3]{0:T(128)S(1)} %pad_add_fusion.scalars_ref.refs_0_, f32[8,256]{1,0:T(8,128)S(1)} %collective-permute-done.7.refs_1_, bf16[256,1024]{1,0:T(8,128)(2,1)S(1)} %collective-permute-done.9.refs_2_, bf16[256,1024]{1,0:T(8,128)(2,1)S(1)} %collective-permute-done.10.refs_3_, ...), custom_call_target="tpu_custom_call" | custom-call | tf_op jit(solution)/shard_map/dispatch/pallas_call | solution.py:224
  72.1 7.3 %all-to-all-start.2 = ((bf16[16,32,2048]{2,1,0:T(8,128)(2,1)}), bf16[16,32,2048]{2,1,0:T(8,128)(2,1)}, u32[]{:S(2)}, u32[]{:S(2)}) async-start(bf16[16,32,2048]{2,1,0:T(8,128)(2,1)} %dispatch.4), calls=%async_computation.2 | async-start | bytes 4194304 | tf_op jit(solution)/shard_map/all_to_all | solution.py:559
  79.4 2.4 collective-permute-start.18
  82.6 24.8 %collective-permute-done.18.refs_2_ = bf16[256,1024]{1,0:T(8,128)(2,1)S(1)} collective-permute-done((bf16[256,1024]{1,0:T(8,128)(2,1)S(1)}, bf16[256,1024]{1,0:T(8,128)(2,1)S(1)}, u32[]{:S(2)}, u32[]{:S(2)}) %collective-permute-start.18) | collective-permute-done | bytes 524320 | tf_op jit(solution)/shard_map/ppermute | solution.py:517
  107.4 2.4 collective-permute-start.17
  109.8 5.2 %collective-permute-done.17.refs_1_ = f32[8,256]{1,0:T(8,128)S(1)} collective-permute-done((f32[8,256]{1,0:T(8,128)S(1)}, f32[8,256]{1,0:T(8,128)S(1)}, u32[]{:S(2)}, u32[]{:S(2)}) %collective-permute-start.17) | collective-permute-done | bytes 8224 | tf_op jit(solution)/shard_map/ppermute | solution.py:517
  115.0 2.2 dispatch.5
  117.2 6.8 %all-to-all-start.4 = ((bf16[16,16,2048]{2,1,0:T(8,128)(2,1)}), bf16[16,16,2048]{2,1,0:T(8,128)(2,1)S(1)}, u32[]{:S(2)}, u32[]{:S(2)}) async-start(bf16[16,16,2048]{2,1,0:T(8,128)(2,1)} %dispatch.5), calls=%async_computation.4 | async-start | bytes 2097152 | tf_op jit(solution)/shard_map/all_to_all | solution.py:559
  124.0 13.9 %expert.4 = bf16[512,2048]{1,0:T(8,128)(2,1)} custom-call(bf16[512,2048]{1,0:T(8,128)(2,1)} %bitcast.17.refs_0_, bf16[352,2048]{1,0:T(8,128)(2,1)} %bitcast.29, bf16[352,2048]{1,0:T(8,128)(2,1)} %bitcast.34, bf16[352,2048]{1,0:T(8,128)(2,1)} %bitcast.38, bf16[352,2048]{1,0:T(8,128)(2,1)} %collective-permute-done.3.refs_4_, ...), custom_call_target="tpu_custom_call" | custom-call | flops 4429185024 | bytes 12845056 | tf_op jit(solution)/shard_map/expert/pallas_call | solution.py:441
  137.9 3.1 %all-to-all-done.4 = bf16[16,16,2048]{2,1,0:T(8,128)(2,1)S(1)} async-done(((bf16[16,16,2048]{2,1,0:T(8,128)(2,1)}), bf16[16,16,2048]{2,1,0:T(8,128)(2,1)S(1)}, u32[]{:S(2)}, u32[]{:S(2)}) %all-to-all-start.4) | async-done | bytes 1048608 | tf_op jit(solution)/shard_map/all_to_all | solution.py:559
  142.0 4.1 %all-to-all-start.3 = ((bf16[16,32,2048]{2,1,0:T(8,128)(2,1)}), bf16[16,32,2048]{2,1,0:T(8,128)(2,1)S(1)}, u32[]{:S(2)}, u32[]{:S(2)}) async-start(bf16[16,32,2048]{2,1,0:T(8,128)(2,1)} %bitcast.46), calls=%async_computation.3 | async-start | bytes 4194304 | tf_op jit(solution)/shard_map/all_to_all | solution.py:559
  146.2 8.4 %expert.5 = bf16[256,2048]{1,0:T(8,128)(2,1)} custom-call(bf16[256,2048]{1,0:T(8,128)(2,1)} %bitcast.44, bf16[352,2048]{1,0:T(8,128)(2,1)} %bitcast.30, bf16[352,2048]{1,0:T(8,128)(2,1)} %bitcast.35, bf16[352,2048]{1,0:T(8,128)(2,1)} %bitcast.39, bf16[352,2048]{1,0:T(8,128)(2,1)} %collective-permute-done.3.refs_4_, ...), custom_call_target="tpu_custom_call" | custom-call | flops 2214592512 | bytes 10747904 | tf_op jit(solution)/shard_map/expert/pallas_call | solution.py:441
  154.6 20.3 %all-to-all-done.3.refs_3_ = bf16[16,32,2048]{2,1,0:T(8,128)(2,1)S(1)} async-done(((bf16[16,32,2048]{2,1,0:T(8,128)(2,1)}), bf16[16,32,2048]{2,1,0:T(8,128)(2,1)S(1)}, u32[]{:S(2)}, u32[]{:S(2)}) %all-to-all-start.3) | async-done | bytes 2097184 | tf_op jit(solution)/shard_map/all_to_all | solution.py:559
  174.9 3.7 %all-to-all-start.5 = ((bf16[16,16,2048]{2,1,0:T(8,128)(2,1)}), bf16[16,16,2048]{2,1,0:T(8,128)(2,1)S(1)}, u32[]{:S(2)}, u32[]{:S(2)}) async-start(bf16[16,16,2048]{2,1,0:T(8,128)(2,1)} %bitcast.43), calls=%async_computation.5 | async-start | bytes 2097152 | tf_op jit(solution)/shard_map/all_to_all | solution.py:559
  178.6 3.0 %combine.4 = (f32[256,1024]{1,0:T(8,128)S(1)}, f32[256,1024]{1,0:T(8,128)S(1)}, bf16[256,2048]{1,0:T(8,128)(2,1)}) custom-call(s32[3]{0:T(128)S(1)} %pad_add_fusion.scalars_ref.refs_0_, f32[8,256]{1,0:T(8,128)S(1)} %collective-permute-done.7.refs_1_, f32[8,256]{1,0:T(8,128)S(1)} %collective-permute-done.8.refs_4_.refs_2_, ...), custom_call_target="tpu_custom_call" | custom-call | tf_op jit(solution)/shard_map/combine/pallas_call | solution.py:280
  183.7 8.4 %expert.3 = bf16[256,2048]{1,0:T(8,128)(2,1)} custom-call(bf16[256,2048]{1,0:T(8,128)(2,1)} %bitcast.41, bf16[352,2048]{1,0:T(8,128)(2,1)} %bitcast.31, bf16[352,2048]{1,0:T(8,128)(2,1)} %bitcast.36, bf16[352,2048]{1,0:T(8,128)(2,1)} %bitcast.40, bf16[352,2048]{1,0:T(8,128)(2,1)} %collective-permute-done.3.refs_4_, ...), custom_call_target="tpu_custom_call" | custom-call | flops 2214592512 | bytes 10747904 | tf_op jit(solution)/shard_map/expert/pallas_call | solution.py:441
  193.5 6.0 %all-to-all-start.1 = ((bf16[16,16,2048]{2,1,0:T(8,128)(2,1)}), bf16[16,16,2048]{2,1,0:T(8,128)(2,1)S(1)}, u32[]{:S(2)}, u32[]{:S(2)}) async-start(bf16[16,16,2048]{2,1,0:T(8,128)(2,1)} %bitcast.42), calls=%async_computation.1 | async-start | bytes 2097152 | tf_op jit(solution)/shard_map/all_to_all | solution.py:559
  199.4 2.3 combine.5
  203.3 2.2 fold.2
  206.2 11.7 %all-to-all-done.1.refs_2_ = bf16[16,16,2048]{2,1,0:T(8,128)(2,1)S(1)} async-done(((bf16[16,16,2048]{2,1,0:T(8,128)(2,1)}), bf16[16,16,2048]{2,1,0:T(8,128)(2,1)S(1)}, u32[]{:S(2)}, u32[]{:S(2)}) %all-to-all-start.1) | async-done | bytes 1048608 | tf_op jit(solution)/shard_map/all_to_all | solution.py:559
  227.8 4.3 %collective-permute-done.21.came_ref = bf16[256,512]{1,0:T(8,128)(2,1)S(1)} collective-permute-done((bf16[256,512]{1,0:T(8,128)(2,1)S(1)}, bf16[256,512]{1,0:T(8,128)(2,1)S(1)}, u32[]{:S(2)}, u32[]{:S(2)}) %collective-permute-start.21) | collective-permute-done | bytes 262176 | tf_op jit(solution)/shard_map/ppermute | solution.py:511
  233.7 6.6 %collective-permute-done.15.home_ref = bf16[256,1024]{1,0:T(8,128)(2,1)S(1)} collective-permute-done((bf16[256,1024]{1,0:T(8,128)(2,1)S(1)}, bf16[256,1024]{1,0:T(8,128)(2,1)S(1)}, u32[]{:S(2)}, u32[]{:S(2)}) %collective-permute-start.15) | collective-permute-done | bytes 524320 | tf_op jit(solution)/shard_map/ppermute | solution.py:527
  241.1 7.6 %collective-permute-start.16 = (bf16[256,512]{1,0:T(8,128)(2,1)S(1)}, bf16[256,512]{1,0:T(8,128)(2,1)S(1)}, u32[]{:S(2)}, u32[]{:S(2)}) collective-permute-start(bf16[256,512]{1,0:T(8,128)(2,1)S(1)} %get-tuple-element.44), channel_id=1, source_target_pairs={{0,128},{64,192},{128,0},{192,64},{1,129},{65,193},{129,1},{193,65... | collective-permute-start | bytes 786440 | tf_op jit(solution)/shard_map/ppermute | solution.py:511
  248.7 10.4 %collective-permute-done.25.refs_3_ = bf16[2,256,512]{2,1,0:T(8,128)(2,1)S(1)} collective-permute-done((bf16[2,256,512]{2,1,0:T(8,128)(2,1)S(1)}, bf16[2,256,512]{2,1,0:T(8,128)(2,1)S(1)}, u32[]{:S(2)}, u32[]{:S(2)}) %collective-permute-start.25) | collective-permute-done | bytes 524320 | tf_op jit(solution)/shard_map/ppermute | solution.py:511
  261.1 4.2 %collective-permute-done.16.came_ref = bf16[256,512]{1,0:T(8,128)(2,1)S(1)} collective-permute-done((bf16[256,512]{1,0:T(8,128)(2,1)S(1)}, bf16[256,512]{1,0:T(8,128)(2,1)S(1)}, u32[]{:S(2)}, u32[]{:S(2)}) %collective-permute-start.16) | collective-permute-done | bytes 262176 | tf_op jit(solution)/shard_map/ppermute | solution.py:511
  (98 shorter events, 38.0 us)
Async XLA Ops:
  9.4 2.1 collective-permute-start
  12.9 14.1 %collective-permute-start.1 = (bf16[256,1024]{1,0:T(8,128)(2,1)S(1)}, bf16[256,1024]{1,0:T(8,128)(2,1)S(1)}, u32[]{:S(2)}, u32[]{:S(2)}) collective-permute-start(bf16[256,1024]{1,0:T(8,128)(2,1)S(1)} %get-tuple-element.31), channel_id=1, source_target_pairs={{0,128},{64,192},{128,0},{192,64},{1,129},{65,193},{129,1},{193,65... | collective-permute-start | bytes 1572872 | tf_op jit(solution)/shard_map/ppermute | solution.py:511
  27.7 2.0 collective-permute-start.2
  30.7 27.7 %collective-permute-start.11 = (bf16[256,1024]{1,0:T(8,128)(2,1)S(1)}, bf16[256,1024]{1,0:T(8,128)(2,1)S(1)}, u32[]{:S(2)}, u32[]{:S(2)}) collective-permute-start(bf16[256,1024]{1,0:T(8,128)(2,1)S(1)} %get-tuple-element.33.refs_2_), channel_id=1, source_target_pairs={{0,3},{1,0},{2,1},{3,2},{4,7},{5,4},{6,5},{7,6},{8,11},{9,8},{10,9... | collective-permute-start | bytes 1572872 | tf_op jit(solution)/shard_map/ppermute | solution.py:517
  36.1 27.0 %collective-permute-start.9 = (bf16[256,1024]{1,0:T(8,128)(2,1)S(1)}, bf16[256,1024]{1,0:T(8,128)(2,1)S(1)}, u32[]{:S(2)}, u32[]{:S(2)}) collective-permute-start(bf16[256,1024]{1,0:T(8,128)(2,1)S(1)} %get-tuple-element.33.refs_2_), channel_id=1, source_target_pairs={{0,1},{1,2},{2,3},{3,0},{4,5},{5,6},{6,7},{7,4},{8,9},{9,10},{10,1... | collective-permute-start | bytes 1572872 | tf_op jit(solution)/shard_map/ppermute | solution.py:517
  38.2 33.9 %all-to-all-start = ((bf16[16,16,2048]{2,1,0:T(8,128)(2,1)}), bf16[16,16,2048]{2,1,0:T(8,128)(2,1)S(1)}, u32[]{:S(2)}, u32[]{:S(2)}) async-start(bf16[16,16,2048]{2,1,0:T(8,128)(2,1)} %dispatch.3), calls=%async_computation | async-start | bytes 2097152 | tf_op jit(solution)/shard_map/all_to_all | solution.py:559
  58.4 10.9 %collective-permute-start.12 = (bf16[256,1024]{1,0:T(8,128)(2,1)S(1)}, bf16[256,1024]{1,0:T(8,128)(2,1)S(1)}, u32[]{:S(2)}, u32[]{:S(2)}) collective-permute-start(bf16[256,1024]{1,0:T(8,128)(2,1)S(1)} %collective-permute-done.11.refs_5_), channel_id=1, source_target_pairs={{0,64},{64,0},{128,192},{192,128},{1,65},{65,1},{129,193},{193,129... | collective-permute-start | bytes 1572872 | tf_op jit(solution)/shard_map/ppermute | solution.py:511
  63.1 6.2 %collective-permute-start.10 = (bf16[256,1024]{1,0:T(8,128)(2,1)S(1)}, bf16[256,1024]{1,0:T(8,128)(2,1)S(1)}, u32[]{:S(2)}, u32[]{:S(2)}) collective-permute-start(bf16[256,1024]{1,0:T(8,128)(2,1)S(1)} %collective-permute-done.9.refs_2_), channel_id=1, source_target_pairs={{0,64},{64,0},{128,192},{192,128},{1,65},{65,1},{129,193},{193,129... | collective-permute-start | bytes 1572872 | tf_op jit(solution)/shard_map/ppermute | solution.py:511
  63.1 4.6 %collective-permute-start.8 = (f32[8,256]{1,0:T(8,128)S(1)}, f32[8,256]{1,0:T(8,128)S(1)}, u32[]{:S(2)}, u32[]{:S(2)}) collective-permute-start(f32[8,256]{1,0:T(8,128)S(1)} %pad_maximum_fusion.refs_1_), channel_id=1, source_target_pairs={{0,3},{1,0},{2,1},{3,2},{4,7},{5,4},{6,5},{7,6},{8,11},{9,8},{10,9... | collective-permute-start | bytes 24584 | tf_op jit(solution)/shard_map/ppermute | solution.py:517
  63.5 5.8 %collective-permute-start.7 = (f32[8,256]{1,0:T(8,128)S(1)}, f32[8,256]{1,0:T(8,128)S(1)}, u32[]{:S(2)}, u32[]{:S(2)}) collective-permute-start(f32[8,256]{1,0:T(8,128)S(1)} %pad_maximum_fusion.refs_1_), channel_id=1, source_target_pairs={{0,1},{1,2},{2,3},{3,0},{4,5},{5,6},{6,7},{7,4},{8,9},{9,10},{10,1... | collective-permute-start | bytes 24584 | tf_op jit(solution)/shard_map/ppermute | solution.py:517
  72.1 45.0 %all-to-all-start.2 = ((bf16[16,32,2048]{2,1,0:T(8,128)(2,1)}), bf16[16,32,2048]{2,1,0:T(8,128)(2,1)}, u32[]{:S(2)}, u32[]{:S(2)}) async-start(bf16[16,32,2048]{2,1,0:T(8,128)(2,1)} %dispatch.4), calls=%async_computation.2 | async-start | bytes 4194304 | tf_op jit(solution)/shard_map/all_to_all | solution.py:559
  79.4 28.0 %collective-permute-start.18 = (bf16[256,1024]{1,0:T(8,128)(2,1)S(1)}, bf16[256,1024]{1,0:T(8,128)(2,1)S(1)}, u32[]{:S(2)}, u32[]{:S(2)}) collective-permute-start(bf16[256,1024]{1,0:T(8,128)(2,1)S(1)} %get-tuple-element.33.refs_2_), channel_id=1, source_target_pairs={{0,2},{1,3},{2,0},{3,1},{4,6},{5,7},{6,4},{7,5},{8,10},{9,11},{10,... | collective-permute-start | bytes 1572872 | tf_op jit(solution)/shard_map/ppermute | solution.py:517
  81.8 42.2 %collective-permute-start.3 = (bf16[352,2048]{1,0:T(8,128)(2,1)S(1)}, bf16[352,2048]{1,0:T(8,128)(2,1)}, u32[]{:S(2)}, u32[]{:S(2)}) collective-permute-start(bf16[352,2048]{1,0:T(8,128)(2,1)S(1)} %bitcast.32), channel_id=1, source_target_pairs={{0,64},{64,0},{128,192},{192,128},{1,65},{65,1},{129,193},{193,129... | collective-permute-start | bytes 4325384 | tf_op jit(solution)/shard_map/ppermute | solution.py:511
  81.8 42.2 %collective-permute-start.4 = (bf16[352,2048]{1,0:T(8,128)(2,1)}, bf16[352,2048]{1,0:T(8,128)(2,1)}, u32[]{:S(2)}, u32[]{:S(2)}) collective-permute-start(bf16[352,2048]{1,0:T(8,128)(2,1)} %bitcast.33), channel_id=1, source_target_pairs={{0,64},{64,0},{128,192},{192,128},{1,65},{65,1},{129,193},{193,129... | collective-permute-start | bytes 4325384 | tf_op jit(solution)/shard_map/ppermute | solution.py:511
  82.3 41.7 %collective-permute-start.5 = (bf16[352,2048]{1,0:T(8,128)(2,1)}, bf16[352,2048]{1,0:T(8,128)(2,1)}, u32[]{:S(2)}, u32[]{:S(2)}) collective-permute-start(bf16[352,2048]{1,0:T(8,128)(2,1)} %bitcast.37), channel_id=1, source_target_pairs={{0,64},{64,0},{128,192},{192,128},{1,65},{65,1},{129,193},{193,129... | collective-permute-start | bytes 4325384 | tf_op jit(solution)/shard_map/ppermute | solution.py:511
  107.4 7.6 %collective-permute-start.19 = (bf16[256,1024]{1,0:T(8,128)(2,1)S(1)}, bf16[256,1024]{1,0:T(8,128)(2,1)S(1)}, u32[]{:S(2)}, u32[]{:S(2)}) collective-permute-start(bf16[256,1024]{1,0:T(8,128)(2,1)S(1)} %collective-permute-done.18.refs_2_), channel_id=1, source_target_pairs={{0,64},{64,0},{128,192},{192,128},{1,65},{65,1},{129,193},{193,129... | collective-permute-start | bytes 1572872 | tf_op jit(solution)/shard_map/ppermute | solution.py:511
  107.4 7.6 %collective-permute-start.17 = (f32[8,256]{1,0:T(8,128)S(1)}, f32[8,256]{1,0:T(8,128)S(1)}, u32[]{:S(2)}, u32[]{:S(2)}) collective-permute-start(f32[8,256]{1,0:T(8,128)S(1)} %pad_maximum_fusion.refs_1_), channel_id=1, source_target_pairs={{0,2},{1,3},{2,0},{3,1},{4,6},{5,7},{6,4},{7,5},{8,10},{9,11},{10,... | collective-permute-start | bytes 24584 | tf_op jit(solution)/shard_map/ppermute | solution.py:517
  117.2 23.8 %all-to-all-start.4 = ((bf16[16,16,2048]{2,1,0:T(8,128)(2,1)}), bf16[16,16,2048]{2,1,0:T(8,128)(2,1)S(1)}, u32[]{:S(2)}, u32[]{:S(2)}) async-start(bf16[16,16,2048]{2,1,0:T(8,128)(2,1)} %dispatch.5), calls=%async_computation.4 | async-start | bytes 2097152 | tf_op jit(solution)/shard_map/all_to_all | solution.py:559
  142.0 32.9 %all-to-all-start.3 = ((bf16[16,32,2048]{2,1,0:T(8,128)(2,1)}), bf16[16,32,2048]{2,1,0:T(8,128)(2,1)S(1)}, u32[]{:S(2)}, u32[]{:S(2)}) async-start(bf16[16,32,2048]{2,1,0:T(8,128)(2,1)} %bitcast.46), calls=%async_computation.3 | async-start | bytes 4194304 | tf_op jit(solution)/shard_map/all_to_all | solution.py:559
  174.9 18.6 %all-to-all-start.5 = ((bf16[16,16,2048]{2,1,0:T(8,128)(2,1)}), bf16[16,16,2048]{2,1,0:T(8,128)(2,1)S(1)}, u32[]{:S(2)}, u32[]{:S(2)}) async-start(bf16[16,16,2048]{2,1,0:T(8,128)(2,1)} %bitcast.43), calls=%async_computation.5 | async-start | bytes 2097152 | tf_op jit(solution)/shard_map/all_to_all | solution.py:559
  183.7 18.3 %collective-permute-start.13 = (bf16[256,2048]{1,0:T(8,128)(2,1)}, bf16[256,2048]{1,0:T(8,128)(2,1)}, u32[]{:S(2)}, u32[]{:S(2)}) collective-permute-start(bf16[256,2048]{1,0:T(8,128)(2,1)} %get-tuple-element.40), channel_id=1, source_target_pairs={{0,64},{64,0},{128,192},{192,128},{1,65},{65,1},{129,193},{193,129... | collective-permute-start | bytes 3145736 | tf_op jit(solution)/shard_map/ppermute | solution.py:511
  193.5 24.4 %all-to-all-start.1 = ((bf16[16,16,2048]{2,1,0:T(8,128)(2,1)}), bf16[16,16,2048]{2,1,0:T(8,128)(2,1)S(1)}, u32[]{:S(2)}, u32[]{:S(2)}) async-start(bf16[16,16,2048]{2,1,0:T(8,128)(2,1)} %bitcast.42), calls=%async_computation.1 | async-start | bytes 2097152 | tf_op jit(solution)/shard_map/all_to_all | solution.py:559
  201.7 17.8 %collective-permute-start.20 = (bf16[256,1024]{1,0:T(8,128)(2,1)}, bf16[256,1024]{1,0:T(8,128)(2,1)}, u32[]{:S(2)}, u32[]{:S(2)}) collective-permute-start(bf16[256,1024]{1,0:T(8,128)(2,1)} %get-tuple-element.47), channel_id=1, source_target_pairs={{0,64},{64,0},{128,192},{192,128},{1,65},{65,1},{129,193},{193,129... | collective-permute-start | bytes 1572872 | tf_op jit(solution)/shard_map/ppermute | solution.py:511
  205.5 18.2 %collective-permute-start.14 = (bf16[256,1024]{1,0:T(8,128)(2,1)}, bf16[256,1024]{1,0:T(8,128)(2,1)}, u32[]{:S(2)}, u32[]{:S(2)}) collective-permute-start(bf16[256,1024]{1,0:T(8,128)(2,1)} %get-tuple-element.42), channel_id=1, source_target_pairs={{0,128},{64,192},{128,0},{192,64},{1,129},{65,193},{129,1},{193,65... | collective-permute-start | bytes 1572872 | tf_op jit(solution)/shard_map/ppermute | solution.py:511
  219.4 12.8 %collective-permute-start.6 = (bf16[256,1024]{1,0:T(8,128)(2,1)S(1)}, bf16[256,1024]{1,0:T(8,128)(2,1)S(1)}, u32[]{:S(2)}, u32[]{:S(2)}) collective-permute-start(bf16[256,1024]{1,0:T(8,128)(2,1)S(1)} %get-tuple-element.37), channel_id=1, source_target_pairs={{0,64},{64,0},{128,192},{192,128},{1,65},{65,1},{129,193},{193,129... | collective-permute-start | bytes 1572872 | tf_op jit(solution)/shard_map/ppermute | solution.py:511
  222.9 9.3 %collective-permute-start.21 = (bf16[256,512]{1,0:T(8,128)(2,1)S(1)}, bf16[256,512]{1,0:T(8,128)(2,1)S(1)}, u32[]{:S(2)}, u32[]{:S(2)}) collective-permute-start(bf16[256,512]{1,0:T(8,128)(2,1)S(1)} %get-tuple-element.49), channel_id=1, source_target_pairs={{0,128},{64,192},{128,0},{192,64},{1,129},{65,193},{129,1},{193,65... | collective-permute-start | bytes 786440 | tf_op jit(solution)/shard_map/ppermute | solution.py:511
  224.8 15.6 %collective-permute-start.15 = (bf16[256,1024]{1,0:T(8,128)(2,1)S(1)}, bf16[256,1024]{1,0:T(8,128)(2,1)S(1)}, u32[]{:S(2)}, u32[]{:S(2)}) collective-permute-start(bf16[256,1024]{1,0:T(8,128)(2,1)S(1)} %total.2), channel_id=1, source_target_pairs={{0,131},{64,195},{128,1},{192,65},{1,128},{65,192},{129,2},{193,66... | collective-permute-start | bytes 1572872 | tf_op jit(solution)/shard_map/ppermute | solution.py:527
  226.3 22.4 %collective-permute-start.23 = (bf16[2,256,512]{2,1,0:T(8,128)(2,1)S(1)}, bf16[2,256,512]{2,1,0:T(8,128)(2,1)S(1)}, u32[]{:S(2)}, u32[]{:S(2)}) collective-permute-start(bf16[2,256,512]{2,1,0:T(8,128)(2,1)S(1)} %get-tuple-element.51), channel_id=1, source_target_pairs={{0,64},{64,0},{128,192},{192,128},{1,65},{65,1},{129,193},{193,129... | collective-permute-start | bytes 1572872 | tf_op jit(solution)/shard_map/ppermute | solution.py:511
  226.5 22.2 %collective-permute-start.24 = (bf16[2,256,512]{2,1,0:T(8,128)(2,1)S(1)}, bf16[2,256,512]{2,1,0:T(8,128)(2,1)S(1)}, u32[]{:S(2)}, u32[]{:S(2)}) collective-permute-start(bf16[2,256,512]{2,1,0:T(8,128)(2,1)S(1)} %get-tuple-element.52), channel_id=1, source_target_pairs={{0,128},{64,192},{128,0},{192,64},{1,129},{65,193},{129,1},{193,65... | collective-permute-start | bytes 1572872 | tf_op jit(solution)/shard_map/ppermute | solution.py:511
  232.1 26.9 %collective-permute-start.25 = (bf16[2,256,512]{2,1,0:T(8,128)(2,1)S(1)}, bf16[2,256,512]{2,1,0:T(8,128)(2,1)S(1)}, u32[]{:S(2)}, u32[]{:S(2)}) collective-permute-start(bf16[2,256,512]{2,1,0:T(8,128)(2,1)S(1)} %get-tuple-element.53), channel_id=1, source_target_pairs={{0,192},{64,128},{128,64},{192,0},{1,193},{65,129},{129,65},{193,1... | collective-permute-start | bytes 1572872 | tf_op jit(solution)/shard_map/ppermute | solution.py:511
  232.2 28.8 %collective-permute-start.22 = (bf16[256,512]{1,0:T(8,128)(2,1)S(1)}, bf16[256,512]{1,0:T(8,128)(2,1)S(1)}, u32[]{:S(2)}, u32[]{:S(2)}) collective-permute-start(bf16[256,512]{1,0:T(8,128)(2,1)S(1)} %total.3), channel_id=1, source_target_pairs={{0,130},{64,194},{128,2},{192,66},{1,131},{65,195},{129,3},{193,67... | collective-permute-start | bytes 786440 | tf_op jit(solution)/shard_map/ppermute | solution.py:527
  241.1 24.2 %collective-permute-start.16 = (bf16[256,512]{1,0:T(8,128)(2,1)S(1)}, bf16[256,512]{1,0:T(8,128)(2,1)S(1)}, u32[]{:S(2)}, u32[]{:S(2)}) collective-permute-start(bf16[256,512]{1,0:T(8,128)(2,1)S(1)} %get-tuple-element.44), channel_id=1, source_target_pairs={{0,128},{64,192},{128,0},{192,64},{1,129},{65,193},{129,1},{193,65... | collective-permute-start | bytes 786440 | tf_op jit(solution)/shard_map/ppermute | solution.py:511
  (20 other events, 133.3 us)
